TPU v7x, 128 devices: a whole 4x4x4 slice. The times are simulated.
128 devices in a mesh: group: 8 (over x_lo, z), tensor: 16 (over x_hi, y, core).
Axes of the slice: x: 4 (x_hi: 2, x_lo: 2; x = x_hi * 2 + x_lo), y: 4, z: 4, core: 2. Of those that a mesh axis runs over, the one named last changes fastest.
Arguments:
- hidden: bfloat16 [12288, 2048], P(('group', 'tensor')), may hold values from -20 to 20
- request_of: int32 [12288], P('group'), may hold values from 0 to 191, as said below
- positions: int32 [12288], P('group'), may hold values from 0 to 511, as said below
- page_table: int32 [8, 64], P('group'), may hold values from 0 to 63, each once within a row
- attn_gain: float32 [2048], replicated, may hold values from 0.5 to 1.5
- mlp_gain: float32 [2048], replicated, may hold values from 0.5 to 1.5
- wq: float32 [2048, 2048], P('group', 'tensor'), may hold values from -2 to 2
- wk: float32 [2048, 1024], P('group', 'tensor'), may hold values from -1 to 1
- wv: float32 [2048, 1024], P('group', 'tensor'), may hold values from -0.125 to 0.125
- wo: float32 [2048, 2048], P('tensor', 'group'), may hold values from -0.125 to 0.125
- w_gate: float32 [2048, 8192], P('group', 'tensor'), may hold values from -0.125 to 0.125
- w_up: float32 [2048, 8192], P('group', 'tensor'), may hold values from -0.125 to 0.125
- w_down: float32 [8192, 2048], P('tensor', 'group'), may hold values from -0.0625 to 0.0625
Outputs:
- layer_out: bfloat16 [12288, 2048], P(('group', 'tensor'))
- kv_pages: bfloat16 [512, 128, 2048], P('group', None, 'tensor')
Inputs may be any that keep to these rules, and one draw needn't show every extreme that they name: `request_of`: prompt numbers rise strictly along the token stream, starting at 0, and the last prompt of the stream has the number 12288 // 64 - 1; a prompt's rows are consecutive, and a prompt that reaches the last row of one block of 1536 rows continues at the first row of the next block. A prompt's rows have positions 0, 1, 2 and so on in order; a prompt has at most 512 rows, and one has exactly 512.
All inputs are finite; a program needn't handle non-finite values.
Results may differ from a plain program's by a relative error of at most 0.014.
Values may be sent and summed in bfloat16 or wider, within the bound.
A program may use at most 128 MiB of HBM per device.

v0:
```python
import functools

import jax
import jax.numpy as jnp
from jax import lax
from jax.experimental import pallas as pl
from jax.experimental.pallas import tpu as pltpu
from jax.sharding import Mesh
from jax.sharding import PartitionSpec as P

QH = 16
KVH = 8
HD = 128
PAGE = 128
MAXLEN = 512


rope_base = 1000000.0
norm_eps = 1e-06


def swap_cores(value):
    return lax.ppermute(value, "core", [(0, 1), (1, 0)])


def from_behind(block, axis, distance):
    devices = range(lax.axis_size(axis))
    route = [(i - distance, i) for i in devices if i - distance in devices]
    return lax.ppermute(block, axis, route)


def exchange_kernel(count, spread, extra, *refs):
    if extra:
        source, weights, slots, weight_slots, send_sems, recv_sems, local_sem = refs
    else:
        source, slots, send_sems, recv_sems, local_sem = refs
    me = lax.axis_index("chip")
    group = lax.axis_index("group")
    core = lax.axis_index("core")
    groups = lax.axis_size("group")
    mesh_ids = pl.DeviceIdType.MESH
    barrier = pltpu.get_barrier_semaphore()
    for shift in range(1, count):
        peer = lax.rem(me + shift, count)
        pl.semaphore_signal(barrier, inc=1, device_id=(group, peer, core), device_id_type=mesh_ids)
    if extra:
        for shift in range(1, groups):
            peer = lax.rem(group + shift, groups)
            pl.semaphore_signal(barrier, inc=1, device_id=(peer, me, core), device_id_type=mesh_ids)
        pl.semaphore_wait(barrier, count - 1 + groups - 1)
    else:
        pl.semaphore_wait(barrier, count - 1)
    local = pltpu.make_async_copy(source.at[me] if spread else source, slots.at[me], local_sem.at[0])
    local.start()
    copies = [local]
    if extra:
        weight_local = pltpu.make_async_copy(weights, weight_slots.at[group], local_sem.at[1])
        weight_local.start()
        copies.append(weight_local)
        for shift in range(1, groups):
            peer = lax.rem(group + shift, groups)
            copy = pltpu.make_async_remote_copy(
                src_ref=weights,
                dst_ref=weight_slots.at[group],
                send_sem=send_sems.at[count + shift],
                recv_sem=recv_sems.at[count + shift],
                device_id=(peer, me, core),
                device_id_type=mesh_ids,
            )
            copy.start()
            copies.append(copy)
    for shift in range(1, count):
        peer = lax.rem(me + shift, count)
        copy = pltpu.make_async_remote_copy(
            src_ref=source.at[peer] if spread else source,
            dst_ref=slots.at[me],
            send_sem=send_sems.at[shift],
            recv_sem=recv_sems.at[shift],
            device_id=(group, peer, core),
            device_id_type=mesh_ids,
        )
        copy.start()
        copies.append(copy)
    for shift in range(1, count):
        sender = lax.rem(me + count - shift, count)
        pltpu.make_async_remote_copy(
            src_ref=slots.at[sender],
            dst_ref=slots.at[sender],
            send_sem=send_sems.at[shift],
            recv_sem=recv_sems.at[shift],
            device_id=(group, sender, core),
            device_id_type=mesh_ids,
        ).wait_recv()
    if extra:
        for shift in range(1, groups):
            sender = lax.rem(group + groups - shift, groups)
            pltpu.make_async_remote_copy(
                src_ref=weight_slots.at[sender],
                dst_ref=weight_slots.at[sender],
                send_sem=send_sems.at[count + shift],
                recv_sem=recv_sems.at[count + shift],
                device_id=(sender, me, core),
                device_id_type=mesh_ids,
            ).wait_recv()
    for copy in copies[:1 + extra]:
        copy.wait()
    for copy in copies[1 + extra:]:
        copy.wait_send()


def exchange(block, spread, tag, weights=None):
    count = lax.axis_size("chip")
    groups = lax.axis_size("group")
    rows, cols = block.shape[-2:]
    moved = count * rows * cols * block.dtype.itemsize
    out_shape = [jax.ShapeDtypeStruct((count, rows, cols), block.dtype)]
    operands = [block]
    extra = weights is not None
    if extra:
        out_shape.append(jax.ShapeDtypeStruct((groups,) + weights.shape, weights.dtype))
        operands.append(weights)
        moved += groups * weights.size * weights.dtype.itemsize
    outs = pl.pallas_call(
        functools.partial(exchange_kernel, count, spread, extra),
        out_shape=tuple(out_shape),
        in_specs=[pl.BlockSpec(memory_space=pl.ANY)] * len(operands),
        out_specs=tuple(pl.BlockSpec(memory_space=pl.ANY) for _ in out_shape),
        scratch_shapes=[
            pltpu.SemaphoreType.DMA((count + groups,)),
            pltpu.SemaphoreType.DMA((count + groups,)),
            pltpu.SemaphoreType.DMA((2,)),
        ],
        compiler_params=pltpu.CompilerParams(collective_id=tag, has_side_effects=True),
        cost_estimate=pl.CostEstimate(flops=0, bytes_accessed=2 * moved, transcendentals=0),
    )(*operands)
    return outs


def gather_chip(block, tag, weights=None):
    outs = exchange(block, False, tag, weights)
    rows = outs[0].reshape(-1, block.shape[1])
    if weights is None:
        return rows
    return rows, outs[1].reshape(-1, weights.shape[1])


def scatter_chip(partial, tag, weights=None):
    count = lax.axis_size("chip")
    outs = exchange(partial.reshape(count, -1, partial.shape[1]), True, tag, weights)
    summed = jnp.sum(outs[0].astype(jnp.float32), axis=0)
    if weights is None:
        return summed
    return summed, outs[1].reshape(-1, weights.shape[1])


def gather_group(block):
    count = lax.axis_size("group")
    pieces = [block]
    for shift in range(1, count):
        route = [(source, (source + shift) % count) for source in range(count)]
        pieces.append(lax.ppermute(block, "group", route))
    stacked = jnp.stack(pieces)
    order = (lax.axis_index("group") - jnp.arange(count)) % count
    return jnp.take(stacked, order, axis=0).reshape(count * block.shape[0], block.shape[1])


def rms_scale(values, gain):
    square = jnp.mean(values * values, axis=-1, keepdims=True)
    return (values * lax.rsqrt(square + norm_eps) * gain).astype(jnp.bfloat16)


def rotate(values, places):
    half_dim = values.shape[-1] // 2
    frequency = rope_base ** (-(jnp.arange(half_dim, dtype=jnp.float32) * 2.0 / values.shape[-1]))
    angle = places.astype(jnp.float32)[:, None] * frequency[None, :]
    cosine = jnp.cos(angle)[:, None, :]
    sine = jnp.sin(angle)[:, None, :]
    widened = values.astype(jnp.float32)
    first = widened[..., :half_dim]
    second = widened[..., half_dim:]
    return jnp.concatenate(
        [first * cosine - second * sine, second * cosine + first * sine], axis=-1
    ).astype(jnp.bfloat16)


def by_core(own_part, other_part):
    first = lax.axis_index("core") == 0
    return jnp.where(first, own_part, other_part), jnp.where(first, other_part, own_part)


def dot(acts, weight):
    return jnp.dot(acts, weight, preferred_element_type=jnp.float32)


def dot_t(acts, weight_t):
    return lax.dot_general(
        acts, weight_t, (((1,), (1,)), ((), ())), preferred_element_type=jnp.float32
    )


def core_rows(values, chips, rows_dev):
    blocks = values.reshape(chips, 2, rows_dev, *values.shape[1:])
    own = lax.dynamic_index_in_dim(blocks, lax.axis_index("core"), axis=1, keepdims=False)
    return own.reshape(chips * rows_dev, *values.shape[1:])


def body(
    hidden,
    request_of,
    positions,
    page_table,
    attn_gain,
    mlp_gain,
    wq,
    wk,
    wv,
    wo,
    w_gate,
    w_up,
    w_down,
):
    chips = lax.axis_size("chip")
    rows_dev = hidden.shape[0]
    tok_group = request_of.shape[0]
    bf = jnp.bfloat16
    residual = hidden.astype(jnp.float32)
    q_cols = wq.shape[1]
    kv_half = wk.shape[1]
    own_attn = jnp.concatenate([wq.astype(bf), wk.astype(bf), wv.astype(bf), wo.astype(bf).T], axis=1)
    normed, own_attn = gather_chip(rms_scale(residual, attn_gain), 0, own_attn)
    other_attn = swap_cores(own_attn)
    query_w = jnp.concatenate([own_attn[:, :q_cols], other_attn[:, :q_cols]], axis=1)
    out_w_t = jnp.concatenate(
        [own_attn[:, q_cols + 2 * kv_half :], other_attn[:, q_cols + 2 * kv_half :]], axis=1
    )
    key_lo, key_hi = by_core(own_attn[:, q_cols : q_cols + kv_half], other_attn[:, q_cols : q_cols + kv_half])
    value_lo, value_hi = by_core(
        own_attn[:, q_cols + kv_half : q_cols + 2 * kv_half],
        other_attn[:, q_cols + kv_half : q_cols + 2 * kv_half],
    )
    key_w = jnp.concatenate([key_lo, key_hi], axis=1)
    value_w = jnp.concatenate([value_lo, value_hi], axis=1)
    ff_cols = w_gate.shape[1]
    own_mlp = jnp.concatenate([w_gate.astype(bf), w_up.astype(bf), w_down.astype(bf).T], axis=1)
    half_pos = core_rows(positions, chips, rows_dev)
    half_req = core_rows(request_of, chips, rows_dev)
    heads = 2 * q_cols // HD
    queries = rotate(dot(normed, query_w).astype(bf).reshape(-1, heads, HD), half_pos)
    keys_half = rotate(dot(normed, key_w).astype(bf).reshape(-1, 1, HD), half_pos)
    values_half = dot(normed, value_w).astype(bf).reshape(-1, 1, HD)
    kv_own = jnp.stack([keys_half[:, 0], values_half[:, 0]], axis=1)
    kv_other = swap_cores(kv_own)
    kv_lo, kv_hi = by_core(kv_own, kv_other)
    kv_rows = jnp.stack(
        [kv_lo.reshape(chips, rows_dev, 2, HD), kv_hi.reshape(chips, rows_dev, 2, HD)], axis=1
    ).reshape(tok_group, 2, HD)
    earlier_rows = min(MAXLEN, tok_group)
    earlier = from_behind(kv_rows[tok_group - earlier_rows :], "group", 1)
    all_rows = jnp.concatenate([earlier, kv_rows], axis=0)
    all_keys = all_rows[:, 0]
    all_values = all_rows[:, 1]
    first_request = request_of[0]
    first_position = positions[0]
    same_local = (half_req[:, None] == request_of[None, :]) & (
        positions[None, :] <= half_pos[:, None]
    )
    same_earlier = (half_req[:, None] == first_request) & (
        jnp.arange(earlier_rows)[None, :] >= earlier_rows - first_position
    )
    visible = jnp.concatenate([same_earlier, same_local], axis=1)
    scores = jnp.einsum(
        "qhd,kd->hqk", queries, all_keys, preferred_element_type=jnp.float32
    ) * HD ** (-0.5)
    scores = jnp.where(visible[None], scores, -1e30)
    row_peak = jnp.max(scores, axis=-1, keepdims=True)
    probs = jnp.where(visible[None], jnp.exp(scores - row_peak), 0.0)
    total = jnp.sum(probs, axis=-1, keepdims=True)
    mixed_heads = jnp.einsum(
        "hqk,kd->qhd", probs.astype(bf), all_values, preferred_element_type=jnp.float32
    ) / jnp.transpose(total, (1, 0, 2))
    attended = mixed_heads.astype(bf).reshape(-1, heads * HD)
    attn_part = dot_t(attended, out_w_t)
    attn_sum, own_mlp = scatter_chip(attn_part.astype(bf), 1, own_mlp)
    other_mlp = swap_cores(own_mlp)
    mixed = residual + attn_sum
    normed_mlp = gather_chip(rms_scale(mixed, mlp_gain), 2)
    gate_sum = jnp.concatenate(
        [dot(normed_mlp, own_mlp[:, :ff_cols]), dot(normed_mlp, other_mlp[:, :ff_cols])], axis=1
    )
    up_sum = jnp.concatenate(
        [
            dot(normed_mlp, own_mlp[:, ff_cols : 2 * ff_cols]),
            dot(normed_mlp, other_mlp[:, ff_cols : 2 * ff_cols]),
        ],
        axis=1,
    )
    activation = (jax.nn.silu(gate_sum) * up_sum).astype(bf)
    down_w_t = jnp.concatenate([own_mlp[:, 2 * ff_cols :], other_mlp[:, 2 * ff_cols :]], axis=1)
    down_part = dot_t(activation, down_w_t)
    layer_out = (mixed + scatter_chip(down_part.astype(bf), 3)).astype(bf)
    pages = page_table.shape[1]
    changed = jnp.concatenate(
        [jnp.ones((1,), jnp.int32), (request_of[1:] != request_of[:-1]).astype(jnp.int32)]
    )
    opens = jnp.maximum(changed, (positions % PAGE == 0).astype(jnp.int32))
    logical = jnp.cumsum(opens) - 1
    chosen = jnp.sum(
        jnp.where(logical[:, None] == jnp.arange(pages)[None, :], page_table, 0), axis=1
    )
    target = chosen * PAGE + positions % PAGE
    own_slice = lax.dynamic_index_in_dim(kv_rows, lax.axis_index("core"), axis=1, keepdims=False)
    width = own_slice.shape[1]
    cache = jnp.zeros((pages * PAGE, width), jnp.bfloat16).at[target].set(own_slice)
    return (layer_out, cache.reshape(pages, PAGE, width))


def solution(mesh):
    groups, tensors = mesh.devices.shape
    split = Mesh(mesh.devices.reshape(groups, tensors // 2, 2), ("group", "chip", "core"))
    tensor = ("chip", "core")
    placed = (
        P(("group",) + tensor, None),
        P("group"),
        P("group"),
        P("group", None),
        P(),
        P(),
        P("group", tensor),
        P("group", tensor),
        P("group", tensor),
        P(tensor, "group"),
        P("group", tensor),
        P("group", tensor),
        P(tensor, "group"),
    )
    return jax.shard_map(
        body,
        mesh=split,
        in_specs=placed,
        out_specs=(P(("group",) + tensor, None), P("group", None, tensor)),
        check_vma=False,
    )
```

profile of v0, /device:TPU:2, one launch (start us, length us, event | category | flops | bytes accessed | tf_op | source)
XLA Modules:
  0.0 419.4 jit_solution(664852310910898222)
XLA Ops:
  5.8 1.9 fusion.49.refs_0_
  8.5 63.4 %shard_map.140 = (bf16[8,96,2048]{2,1,0:T(8,128)(2,1)}, bf16[8,256,384]{2,1,0:T(8,128)(2,1)}) custom-call(bf16[96,2048]{1,0:T(8,128)(2,1)} %fusion.49.refs_0_, bf16[256,384]{1,0:T(8,128)(2,1)} %pad_maximum_fusion.6.refs_1_), custom_call_target="tpu_custom_call" | custom-call | bytes 9437184 | tf_op jit(solution)/shard_map/pallas_call | solution.py:123
  72.8 1.2 slice.90
  74.8 1.2 slice.91
  77.1 2.5 multiply_cosine_fusion
  81.5 1.4 compare_and_fusion
  82.9 1.7 pad_add_fusion
  85.1 1.4 copy-done
  86.5 1.3 fusion.37
  88.5 1.3 fusion.38
  93.3 1.3 copy.66
  94.6 1.9 broadcast_select_fusion.5
  96.5 1.9 copy.53
  99.3 1.2 pad_maximum_fusion.1
  100.6 6.4 %collective-permute-start.2 = (bf16[512,2,128]{2,0,1:T(8,128)(2,1)S(1)}, bf16[512,2,128]{2,0,1:T(8,128)(2,1)S(1)}, u32[]{:S(2)}, u32[]{:S(2)}) collective-permute-start(bf16[512,2,128]{2,0,1:T(8,128)(2,1)S(1)} %slice.115), channel_id=1, source_target_pairs={{0,16},{16,32},{32,48},{48,64},{64,80},{80,96},{96,112},{1,17},{17... | collective-permute-start | bytes 786440 | tf_op jit(solution)/shard_map/ppermute | solution.py:29
  107.0 2.2 subtract_convert_fusion
  109.3 10.6 %collective-permute-done.2 = bf16[512,2,128]{2,0,1:T(8,128)(2,1)S(1)} collective-permute-done((bf16[512,2,128]{2,0,1:T(8,128)(2,1)S(1)}, bf16[512,2,128]{2,0,1:T(8,128)(2,1)S(1)}, u32[]{:S(2)}, u32[]{:S(2)}) %collective-permute-start.2) | collective-permute-done | bytes 262176 | tf_op jit(solution)/shard_map/ppermute | solution.py:29
  120.6 10.4 %fusion.95 = (f32[2,768]{1,0:T(2,128)S(1)}, bf16[2,768,2048]{1,2,0:T(8,128)(2,1)}) fusion(pred[768,2048]{0,1:T(8,128)(4,1)} %pad_add_fusion, bf16[1536,2,128]{2,0,1:T(8,128)(2,1)S(1)} %bitcast.98, bf16[512,2,128]{2,0,1:T(8,128)(2,1)} %copy-done.12, bf16[768,2,64]{2,0,1:T(8,128)(2,1)} %get-tuple-element.15, bf16[768,2,64]{2,0,1:T(8,128)(2,1)} %get-tuple-element.14), kind=kOutput, calls=%fused_computation.135 | convolution fusion | flops 826017792 | bytes 9312256 | tf_op jit(solution)/shard_map/sub | solution.py:276
  131.1 3.8 fusion.33
  134.9 2.7 convolution_convert_fusion
  137.6 139.2 %shard_map.141 = (bf16[8,96,2048]{2,1,0:T(8,128)(2,1)}, bf16[8,256,1536]{2,1,0:T(8,128)(2,1)}) custom-call(bf16[8,96,2048]{2,1,0:T(8,128)(2,1)} %bitcast.85, bf16[256,1536]{1,0:T(8,128)(2,1)} %pad_maximum_fusion.2.refs_1_), custom_call_target="tpu_custom_call" | custom-call | bytes 18874368 | tf_op jit(solution)/shard_map/pallas_call | solution.py:123
  277.8 6.1 %scatter_custom_fusion = bf16[8192,128]{1,0:T(8,128)(2,1)} fusion(s32[1536]{0:T(1024)S(1)} %compare_select_fusion, bf16[]{:T(256)} %constant.70.clone.1, bf16[1536,2,128]{2,0,1:T(8,128)(2,1)S(1)} %bitcast.100, s32[]{:T(128)} %constant.58.clone.1, s32[]{:T(128)S(6)} %select_n.66), kind=kCustom, calls=%fused_computation.53 | custom fusion | bytes 2490378 | tf_op jit(solution)/shard_map/scatter | solution.py:313
  283.9 1.9 slice.128
  288.1 55.5 %shard_map.142 = bf16[8,96,2048]{2,1,0:T(8,128)(2,1)} custom-call(bf16[96,2048]{1,0:T(8,128)(2,1)} %multiply_convert_fusion.refs_0_), custom_call_target="tpu_custom_call" | custom-call | bytes 6291456 | tf_op jit(solution)/shard_map/pallas_call | solution.py:123
  343.6 4.5 %fusion.21 = f32[768,512]{0,1:T(8,128)S(1)} fusion(bf16[768,2048]{1,0:T(8,128)(2,1)} %bitcast.89, bf16[2048,1536]{1,0:T(8,128)(2,1)} %bitcast.109), kind=kOutput, calls=%fused_computation.29 | convolution fusion | flops 1610612736 | bytes 6815744 | tf_op jit(solution)/shard_map/dot_general | solution.py:192
  348.2 3.4 fusion.17
  351.6 3.4 fusion.19
  355.1 3.4 fusion.15
  358.5 1.7 slice.129
  360.3 5.2 %fusion.11 = bf16[768,2048]{1,0:T(8,128)(2,1)} fusion(bf16[2048,512]{1,0:T(8,128)(2,1)S(1)} %slice.129, bf16[2048,512]{1,0:T(8,128)(2,1)S(1)} %slice.128, f32[768,512]{0,1:T(8,128)S(1)} %fusion.15, f32[768,512]{0,1:T(8,128)S(1)} %fusion.17, f32[768,512]{0,1:T(8,128)S(1)} %fusion.19, f32[768,512]{0,1:T(8,128)S(1)} %fusion.21), kind=kOutput, calls=%fused_computation.18 | convolution fusion | flops 3237478400 | bytes 13631488 | tf_op jit(solution)/shard_map/dot_general | solution.py:196
  365.4 50.5 %shard_map.143 = bf16[8,96,2048]{2,1,0:T(8,128)(2,1)} custom-call(bf16[8,96,2048]{2,1,0:T(8,128)(2,1)} %bitcast.93), custom_call_target="tpu_custom_call" | custom-call | bytes 6291456 | tf_op jit(solution)/shard_map/pallas_call | solution.py:123
  416.0 2.5 convert_reduce_fusion
  (81 shorter events, 20.5 us)
Async XLA Ops:
  0.6 76.2 %copy-start.5 = (f32[512,256]{1,0:T(8,128)S(1)}, f32[512,256]{1,0:T(8,128)}, u32[]{:S(2)}) copy-start(f32[512,256]{1,0:T(8,128)} %param.25) | copy-start | bytes 1572868
  0.6 76.4 %copy-start.6 = (f32[256,512]{1,0:T(8,128)S(1)}, f32[256,512]{1,0:T(8,128)}, u32[]{:S(2)}) copy-start(f32[256,512]{1,0:T(8,128)} %param.23) | copy-start | bytes 1572868
  0.7 76.4 %copy-start.7 = (f32[256,512]{1,0:T(8,128)S(1)}, f32[256,512]{1,0:T(8,128)}, u32[]{:S(2)}) copy-start(f32[256,512]{1,0:T(8,128)} %param.24) | copy-start | bytes 1572868
  7.8 73.7 %copy-start.8 = (s32[1536]{0:T(1024)S(1)}, s32[1536]{0:T(1024)}, u32[]{:S(2)}) copy-start(s32[1536]{0:T(1024)} %param.15) | copy-start | bytes 18436
  7.8 73.7 %copy-start.9 = (s32[1536]{0:T(1024)S(1)}, s32[1536]{0:T(1024)}, u32[]{:S(2)}) copy-start(s32[1536]{0:T(1024)} %param.14) | copy-start | bytes 18436
  71.9 12.7 %collective-permute-start = (bf16[2048,384]{1,0:T(8,128)(2,1)}, bf16[2048,384]{1,0:T(8,128)(2,1)S(1)}, u32[]{:S(2)}, u32[]{:S(2)}) collective-permute-start(bf16[2048,384]{1,0:T(8,128)(2,1)} %bitcast.94), channel_id=1, source_target_pairs={{0,1},{1,0},{2,3},{3,2},{4,5},{5,4},{6,7},{7,6},{8,9},{9,8},{10,11... | collective-permute-start | bytes 4718600 | tf_op jit(solution)/shard_map/ppermute | solution.py:23
  80.3 4.3 %copy-start.4 = (bf16[8,256,384]{2,1,0:T(8,128)(2,1)S(1)}, bf16[8,256,384]{2,1,0:T(8,128)(2,1)}, u32[]{:S(2)}) copy-start(bf16[8,256,384]{2,1,0:T(8,128)(2,1)} %get-tuple-element.7) | copy-start | bytes 4718596
  84.6 1.9 copy-start
  90.6 4.0 collective-permute-start.1
  100.6 19.3 %collective-permute-start.2 = (bf16[512,2,128]{2,0,1:T(8,128)(2,1)S(1)}, bf16[512,2,128]{2,0,1:T(8,128)(2,1)S(1)}, u32[]{:S(2)}, u32[]{:S(2)}) collective-permute-start(bf16[512,2,128]{2,0,1:T(8,128)(2,1)S(1)} %slice.115), channel_id=1, source_target_pairs={{0,16},{16,32},{32,48},{48,64},{64,80},{80,96},{96,112},{1,17},{17... | collective-permute-start | bytes 786440 | tf_op jit(solution)/shard_map/ppermute | solution.py:29
  119.9 0.7 copy-start.12
  120.6 10.4 %copy-start.13 = (bf16[512,2,128]{2,0,1:T(8,128)(2,1)S(1)}, bf16[512,2,128]{2,0,1:T(8,128)(2,1)}, u32[]{:S(2)}) copy-start(bf16[512,2,128]{2,0,1:T(8,128)(2,1)} %copy-done.12) | copy-start | bytes 786436
  137.6 140.0 %copy-start.11 = (s32[1,64]{1,0:T(1,128)S(1)}, s32[1,64]{1,0:T(1,128)}, u32[]{:S(2)}) copy-start(s32[1,64]{1,0:T(1,128)} %param.16) | copy-start | bytes 772
  276.8 74.8 %collective-permute-start.3 = (bf16[2048,1536]{1,0:T(8,128)(2,1)}, bf16[2048,1536]{1,0:T(8,128)(2,1)}, u32[]{:S(2)}, u32[]{:S(2)}) collective-permute-start(bf16[2048,1536]{1,0:T(8,128)(2,1)} %bitcast.107), channel_id=1, source_target_pairs={{0,1},{1,0},{2,3},{3,2},{4,5},{5,4},{6,7},{7,6},{8,9},{9,8},{10,11... | collective-permute-start | bytes 18874376 | tf_op jit(solution)/shard_map/ppermute | solution.py:23
  283.9 2.5 copy-start.3
  283.9 3.1 copy-start.1
  285.8 1.4 copy-start.10
  343.6 4.6 %copy-start.2 = (bf16[8,96,2048]{2,1,0:T(8,128)(2,1)S(1)}, bf16[8,96,2048]{2,1,0:T(8,128)(2,1)}, u32[]{:S(2)}) copy-start(bf16[8,96,2048]{2,1,0:T(8,128)(2,1)} %shard_map.142) | copy-start | bytes 9437188
where the time goes:
time: 428 us; the launch traced here: 419 us
  Pallas kernels  309 us (72%)
  matrix products  40.6 us (9%)
  other arithmetic  27.2 us (6%)
  local copies, waits for them, and re-layouts  23.6 us (6%)
  waiting for transfers between devices  10.7 us (2%)
  starting transfers between devices  7.06 us (2%)
    pallas_call x4, Pallas kernels, exchange(): pl.pallas_call(functools.partial(exchange_kernel, count, spread, extra),...  309 us
    dot_general x7, matrix products, dot(): return jnp.dot(acts, weight, preferred_element_type=jnp.float32)  18.4 us
    ppermute x1, waiting for transfers between devices, from_behind(): return lax.ppermute(block, axis, route)  10.6 us
    sub x1, matrix products, body(): probs = jnp.where(visible[None], jnp.exp(scores - row_peak), 0.0)  10.4 us
  transfers between devices with their start and end apart: 4, of which 1 were waited for; matrix products, arithmetic and copies ran while one was open for 9% of the time, Pallas kernels for 13%

commit v1 on v0

--- a/solution.py
+++ b/solution.py
@@ -227,7 +227,8 @@
     q_cols = wq.shape[1]
     kv_half = wk.shape[1]
     own_attn = jnp.concatenate([wq.astype(bf), wk.astype(bf), wv.astype(bf), wo.astype(bf).T], axis=1)
-    normed, own_attn = gather_chip(rms_scale(residual, attn_gain), 0, own_attn)
+    own_attn = lax.all_gather(own_attn, "group", axis=0, tiled=True)
+    normed = gather_chip(rms_scale(residual, attn_gain), 0)
     other_attn = swap_cores(own_attn)
     query_w = jnp.concatenate([own_attn[:, :q_cols], other_attn[:, :q_cols]], axis=1)
     out_w_t = jnp.concatenate(
@@ -242,6 +243,7 @@
     value_w = jnp.concatenate([value_lo, value_hi], axis=1)
     ff_cols = w_gate.shape[1]
     own_mlp = jnp.concatenate([w_gate.astype(bf), w_up.astype(bf), w_down.astype(bf).T], axis=1)
+    own_mlp = lax.all_gather(own_mlp, "group", axis=0, tiled=True)
     half_pos = core_rows(positions, chips, rows_dev)
     half_req = core_rows(request_of, chips, rows_dev)
     heads = 2 * q_cols // HD
@@ -280,8 +282,8 @@
     ) / jnp.transpose(total, (1, 0, 2))
     attended = mixed_heads.astype(bf).reshape(-1, heads * HD)
     attn_part = dot_t(attended, out_w_t)
-    attn_sum, own_mlp = scatter_chip(attn_part.astype(bf), 1, own_mlp)
     other_mlp = swap_cores(own_mlp)
+    attn_sum = scatter_chip(attn_part.astype(bf), 1)
     mixed = residual + attn_sum
     normed_mlp = gather_chip(rms_scale(mixed, mlp_gain), 2)
     gate_sum = jnp.concatenate(

time: 428 us -> 368 us (0.86)
  Pallas kernels: 309 us -> 190 us
  waiting for transfers between devices: 10.7 us -> 62.7 us
  between operations: 1.74 us -> 15.1 us
    pallas_call x4, Pallas kernels: 309 us -> 190 us  [exchange(): pl.pallas_call(functools.partial(exchange_kernel, count, spread, extra),...]
    all_gather x0 -> x2, waiting for transfers between devices: none -> 57.6 us  [the longest x1 57.6 us: body(): own_mlp = lax.all_gather(own_mlp, 'group', axis=0, tiled=True)]
    ppermute x1, waiting for transfers between devices: 10.6 us -> 2.12 us  [from_behind(): return lax.ppermute(block, axis, route)]
  transfers between devices with their start and end apart: 4 -> 6, of which waited for: 1 -> 3; matrix products, arithmetic and copies ran while one was open for 9% -> 19% of each run, Pallas kernels for 13% -> 41%
where the time goes in v1:
time: 368 us; the launch traced here: 363 us
  Pallas kernels  190 us (52%)
  waiting for transfers between devices  62.7 us (17%)
  matrix products  41.4 us (11%)
  other arithmetic  29.6 us (8%)
  local copies, waits for them, and re-layouts  20.2 us (5%)
  between operations  15.1 us (4%)
  starting transfers between devices  3.88 us (1%)
    pallas_call x4, Pallas kernels, exchange(): pl.pallas_call(functools.partial(exchange_kernel, count, spread, extra),...  190 us
    all_gather x1, waiting for transfers between devices, body(): own_mlp = lax.all_gather(own_mlp, 'group', axis=0, tiled=True)  57.6 us
    dot_general x7, matrix products, dot(): return jnp.dot(acts, weight, preferred_element_type=jnp.float32)  19.1 us
    sub x1, matrix products, body(): probs = jnp.where(visible[None], jnp.exp(scores - row_peak), 0.0)  10.4 us
    dot_general x2, matrix products, dot_t(): lax.dot_general(acts, weight_t, (((1,), (1,)), ((), ())), preferred_eleme...  7.92 us
  transfers between devices with their start and end apart: 6, of which 3 were waited for; matrix products, arithmetic and copies ran while one was open for 19% of the time, Pallas kernels for 41%

profile of v1, /device:TPU:2, one launch (start us, length us, event | category | flops | bytes accessed | tf_op | source)
XLA Modules:
  0.0 362.7 jit_solution(11054563668678716389)
XLA Ops:
  11.7 1.2 copy.44
  12.9 1.2 copy.45
  18.4 56.5 %shard_map.140 = bf16[8,96,2048]{2,1,0:T(8,128)(2,1)} custom-call(bf16[96,2048]{1,0:T(8,128)(2,1)} %fusion.49.refs_0_), custom_call_target="tpu_custom_call" | custom-call | bytes 6291456 | tf_op jit(solution)/shard_map/pallas_call | solution.py:123
  78.3 2.5 multiply_cosine_fusion
  80.8 1.4 compare_and_fusion
  82.2 2.8 pad_add_fusion
  85.0 1.1 fusion.92
  87.5 1.9 fusion.37
  89.4 57.6 %all-gather.5.cloned.1.call-done = bf16[2048,1536]{0,1:T(8,128)(2,1)} async-done(((bf16[256,1536]{0,1:T(8,128)(2,1)}), bf16[2048,1536]{0,1:T(8,128)(2,1)}) %all-gather.5.cloned.1.call-update) | async-done | bytes 6291472 | tf_op jit(solution)/shard_map/all_gather | solution.py:246
  146.9 1.8 fusion.67
  148.8 2.4 fusion.38
  155.1 3.0 collective-permute-done.1
  158.0 1.3 broadcast_select_fusion.1
  162.3 3.3 collective-permute-start.2
  165.6 1.1 subtract_convert_fusion
  166.7 6.1 %scatter_custom_fusion = bf16[8192,128]{1,0:T(8,128)(2,1)} fusion(s32[1536]{0:T(1024)S(1)} %compare_select_fusion, bf16[]{:T(256)} %constant.70.clone.1, bf16[1536,2,128]{2,0,1:T(8,128)(2,1)S(1)} %bitcast.91, s32[]{:T(128)} %constant.58.clone.1, s32[]{:T(128)S(6)} %select_n.66), kind=kCustom, calls=%fused_computation.53 | custom fusion | bytes 2490378 | tf_op jit(solution)/shard_map/scatter | solution.py:315
  172.9 2.1 collective-permute-done.2
  175.0 10.4 %fusion.95 = (f32[2,768]{1,0:T(2,128)S(1)}, bf16[2,768,2048]{1,2,0:T(8,128)(2,1)}) fusion(pred[768,2048]{0,1:T(8,128)(4,1)} %pad_add_fusion, bf16[1536,2,128]{2,0,1:T(8,128)(2,1)S(1)} %bitcast.92, bf16[512,2,128]{2,0,1:T(8,128)(2,1)} %collective-permute-done.2, bf16[768,2,64]{2,0,1:T(8,128)(2,1)} %get-tuple-element.7, bf16[768,2,64]{2,0,1:T(8,128)(2,1)} %get-tuple-element.6), kind=kOutput, calls=%fused_computation.135 | convolution fusion | flops 826017792 | bytes 9312256 | tf_op jit(solution)/shard_map/sub | solution.py:278
  185.4 4.0 %fusion.33 = bf16[768,2,128]{0,2,1:T(8,128)(2,1)S(1)} fusion(bf16[2,768,2048]{1,2,0:T(8,128)(2,1)} %get-tuple-element.21, bf16[512,2,128]{2,0,1:T(8,128)(2,1)} %collective-permute-done.2, bf16[1536,2,128]{2,0,1:T(8,128)(2,1)S(1)} %bitcast.93, f32[768,2]{0,1:T(2,128)S(1)} %bitcast.100), kind=kOutput, calls=%fused_computation.35 | convolution fusion | flops 806748160 | bytes 7739392 | tf_op jit(solution)/shard_map/hqk,kd->qhd/dot_general | solution.py:280
  189.4 2.7 convolution_convert_fusion
  192.1 45.3 %shard_map.141 = bf16[8,96,2048]{2,1,0:T(8,128)(2,1)} custom-call(bf16[8,96,2048]{2,1,0:T(8,128)(2,1)} %bitcast.81), custom_call_target="tpu_custom_call" | custom-call | bytes 6291456 | tf_op jit(solution)/shard_map/pallas_call | solution.py:123
  237.5 2.5 convert_reduce_fusion.1
  241.1 46.6 %shard_map.142 = bf16[8,96,2048]{2,1,0:T(8,128)(2,1)} custom-call(bf16[96,2048]{1,0:T(8,128)(2,1)} %multiply_convert_fusion.refs_0_), custom_call_target="tpu_custom_call" | custom-call | bytes 6291456 | tf_op jit(solution)/shard_map/pallas_call | solution.py:123
  287.7 1.9 slice.128
  290.2 3.4 fusion.21
  293.7 3.4 fusion.17
  297.2 3.4 fusion.19
  300.6 3.4 fusion.15
  304.1 1.7 slice.129
  305.8 5.2 %fusion.11 = bf16[768,2048]{1,0:T(8,128)(2,1)} fusion(bf16[2048,512]{0,1:T(8,128)(2,1)S(1)} %slice.129, bf16[2048,512]{0,1:T(8,128)(2,1)S(1)} %slice.128, f32[768,512]{0,1:T(8,128)S(1)} %fusion.15, f32[768,512]{0,1:T(8,128)S(1)} %fusion.17, f32[768,512]{0,1:T(8,128)S(1)} %fusion.19, f32[768,512]{0,1:T(8,128)S(1)} %fusion.21), kind=kOutput, calls=%fused_computation.18 | convolution fusion | flops 3237478400 | bytes 13631488 | tf_op jit(solution)/shard_map/dot_general | solution.py:196
  311.0 41.4 %shard_map.143 = bf16[8,96,2048]{2,1,0:T(8,128)(2,1)} custom-call(bf16[8,96,2048]{2,1,0:T(8,128)(2,1)} %bitcast.89), custom_call_target="tpu_custom_call" | custom-call | bytes 6291456 | tf_op jit(solution)/shard_map/pallas_call | solution.py:123
  352.5 2.5 convert_reduce_fusion
  (95 shorter events, 22.3 us)
Async XLA Ops:
  7.2 8.9 %copy-start.15 = (s32[1536]{0:T(1024)S(1)}, s32[1536]{0:T(1024)}, u32[]{:S(2)}) copy-start(s32[1536]{0:T(1024)} %param.14) | copy-start | bytes 18436
  7.2 9.5 %copy-start.14 = (s32[1536]{0:T(1024)S(1)}, s32[1536]{0:T(1024)}, u32[]{:S(2)}) copy-start(s32[1536]{0:T(1024)} %param.15) | copy-start | bytes 18436
  7.2 10.1 %copy-start = (bf16[96,2048]{1,0:T(8,128)(2,1)S(1)}, bf16[96,2048]{1,0:T(8,128)(2,1)}, u32[]{:S(2)}) copy-start(bf16[96,2048]{1,0:T(8,128)(2,1)} %param.13) | copy-start | bytes 1179652
  7.2 10.3 %copy-start.16 = (f32[2048]{0:T(1024)S(1)}, f32[2048]{0:T(1024)}, u32[]{:S(2)}) copy-start(f32[2048]{0:T(1024)} %param.17) | copy-start | bytes 24580
  7.2 73.6 %all-gather.3.cloned.1.call-start = ((), (), s32[]{:S(2)}) async-start(), calls=%async_computation | async-start | bytes 1769472 | tf_op jit(solution)/shard_map/all_gather | solution.py:230
  11.6 135.3 %all-gather.5.cloned.1.call-start = ((), (), s32[]{:S(2)}) async-start(), calls=%async_computation.1 | async-start | bytes 7077888 | tf_op jit(solution)/shard_map/all_gather | solution.py:246
  16.1 60.4 %copy-start.18 = (s32[1,64]{1,0:T(1,128)S(1)}, s32[1,64]{1,0:T(1,128)}, u32[]{:S(2)}) copy-start(s32[1,64]{1,0:T(1,128)} %param.16) | copy-start | bytes 772
  80.8 4.3 %copy-start.5 = (bf16[2048,384]{0,1:T(8,128)(2,1)S(1)}, bf16[2048,384]{0,1:T(8,128)(2,1)}, u32[]{:S(2)}) copy-start(bf16[2048,384]{0,1:T(8,128)(2,1)} %all-gather.3.cloned.1.call-done) | copy-start | bytes 4718596
  80.8 5.4 %collective-permute-start = (bf16[2048,384]{0,1:T(8,128)(2,1)}, bf16[2048,384]{0,1:T(8,128)(2,1)S(1)}, u32[]{:S(2)}, u32[]{:S(2)}) collective-permute-start(bf16[2048,384]{0,1:T(8,128)(2,1)} %all-gather.3.cloned.1.call-done), channel_id=1, source_target_pairs={{0,1},{1,0},{2,3},{3,2},{4,5},{5,4},{6,7},{7,6},{8,9},{9,8},{10,11... | collective-permute-start | bytes 4718600 | tf_op jit(solution)/shard_map/ppermute | solution.py:23
  82.2 5.3 %copy-start.1 = (bf16[8,96,2048]{2,1,0:T(8,128)(2,1)S(1)}, bf16[8,96,2048]{2,1,0:T(8,128)(2,1)}, u32[]{:S(2)}) copy-start(bf16[8,96,2048]{2,1,0:T(8,128)(2,1)} %shard_map.140) | copy-start | bytes 9437188
  86.1 1.3 copy-start.6
  146.9 150.2 %collective-permute-start.3 = (bf16[2048,1536]{0,1:T(8,128)(2,1)}, bf16[2048,1536]{0,1:T(8,128)(2,1)}, u32[]{:S(2)}, u32[]{:S(2)}) collective-permute-start(bf16[2048,1536]{0,1:T(8,128)(2,1)} %all-gather.5.cloned.1.call-done), channel_id=1, source_target_pairs={{0,1},{1,0},{2,3},{3,2},{4,5},{5,4},{6,7},{7,6},{8,9},{9,8},{10,11... | collective-permute-start | bytes 18874376 | tf_op jit(solution)/shard_map/ppermute | solution.py:23
  148.8 3.2 copy-start.10
  148.8 3.2 copy-start.11
  148.8 3.7 %copy-start.7 = (bf16[2048,384]{0,1:T(8,128)(2,1)S(1)}, bf16[2048,384]{0,1:T(8,128)(2,1)}, u32[]{:S(2)}) copy-start(bf16[2048,384]{0,1:T(8,128)(2,1)} %copy-done.6) | copy-start | bytes 4718596
  148.8 4.6 %copy-start.13 = (bf16[2048,128]{0,1:T(8,128)(2,1)S(1)}, bf16[2048,128]{0,1:T(8,128)(2,1)}, u32[]{:S(2)}) copy-start(bf16[2048,128]{0,1:T(8,128)(2,1)} %get-tuple-element.9) | copy-start | bytes 1572868
  151.2 2.2 copy-start.12
  152.0 6.0 %collective-permute-start.1 = (bf16[768,2,128]{0,2,1:T(8,128)(2,1)}, bf16[768,2,128]{0,2,1:T(8,128)(2,1)}, u32[]{:S(2)}, u32[]{:S(2)}) collective-permute-start(bf16[768,2,128]{0,2,1:T(8,128)(2,1)} %pad_maximum_fusion.4), channel_id=1, source_target_pairs={{0,1},{1,0},{2,3},{3,2},{4,5},{5,4},{6,7},{7,6},{8,9},{9,8},{10,11... | collective-permute-start | bytes 1179656 | tf_op jit(solution)/shard_map/ppermute | solution.py:23
  155.0 10.6 %copy-start.8 = (f32[768,64]{1,0:T(8,128)S(1)}, f32[768,64]{1,0:T(8,128)}, u32[]{:S(2)}) copy-start(f32[768,64]{1,0:T(8,128)} %get-tuple-element.18) | copy-start | bytes 589828
  155.0 10.6 %copy-start.9 = (f32[768,64]{1,0:T(8,128)S(1)}, f32[768,64]{1,0:T(8,128)}, u32[]{:S(2)}) copy-start(f32[768,64]{1,0:T(8,128)} %get-tuple-element.19) | copy-start | bytes 589828
  162.3 12.7 %collective-permute-start.2 = (bf16[512,2,128]{2,0,1:T(8,128)(2,1)}, bf16[512,2,128]{2,0,1:T(8,128)(2,1)}, u32[]{:S(2)}, u32[]{:S(2)}) collective-permute-start(bf16[512,2,128]{2,0,1:T(8,128)(2,1)} %slice.115), channel_id=1, source_target_pairs={{0,16},{16,32},{32,48},{48,64},{64,80},{80,96},{96,112},{1,17},{17... | collective-permute-start | bytes 786440 | tf_op jit(solution)/shard_map/ppermute | solution.py:29
  185.4 4.0 %copy-start.3 = (bf16[2048,128]{0,1:T(8,128)(2,1)S(1)}, bf16[2048,128]{0,1:T(8,128)(2,1)}, u32[]{:S(2)}) copy-start(bf16[2048,128]{0,1:T(8,128)(2,1)} %get-tuple-element.8) | copy-start | bytes 1572868
  185.4 4.0 %copy-start.4 = (bf16[2048,128]{0,1:T(8,128)(2,1)S(1)}, bf16[2048,128]{0,1:T(8,128)(2,1)}, u32[]{:S(2)}) copy-start(bf16[2048,128]{0,1:T(8,128)(2,1)} %get-tuple-element.10) | copy-start | bytes 1572868
  237.4 2.7 copy-start.17
  287.7 2.5 copy-start.2
Sparse Core Ops, SparseCore 0:
  11.7 48.0 all-gather.2
  61.4 85.4 all-gather.4

commit v2 on v0

--- a/solution.py
+++ b/solution.py
@@ -29,11 +29,13 @@
     return lax.ppermute(block, axis, route)
 
 
-def exchange_kernel(count, spread, extra, *refs):
-    if extra:
-        source, weights, slots, weight_slots, send_sems, recv_sems, local_sem = refs
-    else:
-        source, slots, send_sems, recv_sems, local_sem = refs
+def exchange_kernel(count, spread, spreads, swaps, *refs):
+    source = refs[0]
+    weights = refs[1] if (spreads or swaps) else None
+    outs = refs[1 + (spreads or swaps) :]
+    slots = outs[0]
+    moved = outs[1] if (spreads or swaps) else None
+    send_sems, recv_sems, local_sem = outs[-3:]
     me = lax.axis_index("chip")
     group = lax.axis_index("group")
     core = lax.axis_index("core")
@@ -43,25 +45,40 @@
     for shift in range(1, count):
         peer = lax.rem(me + shift, count)
         pl.semaphore_signal(barrier, inc=1, device_id=(group, peer, core), device_id_type=mesh_ids)
-    if extra:
+    greeted = count - 1
+    if swaps:
+        pl.semaphore_signal(barrier, inc=1, device_id=(group, me, 1 - core), device_id_type=mesh_ids)
+        greeted += 1
+    if spreads:
         for shift in range(1, groups):
             peer = lax.rem(group + shift, groups)
             pl.semaphore_signal(barrier, inc=1, device_id=(peer, me, core), device_id_type=mesh_ids)
-        pl.semaphore_wait(barrier, count - 1 + groups - 1)
-    else:
-        pl.semaphore_wait(barrier, count - 1)
+        greeted += groups - 1
+    pl.semaphore_wait(barrier, greeted)
     local = pltpu.make_async_copy(source.at[me] if spread else source, slots.at[me], local_sem.at[0])
     local.start()
-    copies = [local]
-    if extra:
-        weight_local = pltpu.make_async_copy(weights, weight_slots.at[group], local_sem.at[1])
-        weight_local.start()
-        copies.append(weight_local)
+    locals_ = [local]
+    copies = []
+    if swaps:
+        swap = pltpu.make_async_remote_copy(
+            src_ref=weights,
+            dst_ref=moved,
+            send_sem=send_sems.at[0],
+            recv_sem=recv_sems.at[0],
+            device_id=(group, me, 1 - core),
+            device_id_type=mesh_ids,
+        )
+        swap.start()
+        copies.append(swap)
+    if spreads:
+        own_weights = pltpu.make_async_copy(weights, moved.at[group], local_sem.at[1])
+        own_weights.start()
+        locals_.append(own_weights)
         for shift in range(1, groups):
             peer = lax.rem(group + shift, groups)
             copy = pltpu.make_async_remote_copy(
                 src_ref=weights,
-                dst_ref=weight_slots.at[group],
+                dst_ref=moved.at[group],
                 send_sem=send_sems.at[count + shift],
                 recv_sem=recv_sems.at[count + shift],
                 device_id=(peer, me, core),
@@ -91,37 +108,40 @@
             device_id=(group, sender, core),
             device_id_type=mesh_ids,
         ).wait_recv()
-    if extra:
+    if swaps:
+        swap.wait_recv()
+    if spreads:
         for shift in range(1, groups):
             sender = lax.rem(group + groups - shift, groups)
             pltpu.make_async_remote_copy(
-                src_ref=weight_slots.at[sender],
-                dst_ref=weight_slots.at[sender],
+                src_ref=moved.at[sender],
+                dst_ref=moved.at[sender],
                 send_sem=send_sems.at[count + shift],
                 recv_sem=recv_sems.at[count + shift],
                 device_id=(sender, me, core),
                 device_id_type=mesh_ids,
             ).wait_recv()
-    for copy in copies[:1 + extra]:
+    for copy in copies:
+        copy.wait_send()
+    for copy in locals_:
         copy.wait()
-    for copy in copies[1 + extra:]:
-        copy.wait_send()
-
-
-def exchange(block, spread, tag, weights=None):
+
+
+def exchange(block, spread, tag, weights=None, spreads=False):
     count = lax.axis_size("chip")
     groups = lax.axis_size("group")
     rows, cols = block.shape[-2:]
     moved = count * rows * cols * block.dtype.itemsize
     out_shape = [jax.ShapeDtypeStruct((count, rows, cols), block.dtype)]
     operands = [block]
-    extra = weights is not None
-    if extra:
-        out_shape.append(jax.ShapeDtypeStruct((groups,) + weights.shape, weights.dtype))
+    swaps = weights is not None and not spreads
+    if weights is not None:
+        copies = groups if spreads else 1
+        out_shape.append(jax.ShapeDtypeStruct((copies,) * spreads + weights.shape, weights.dtype))
         operands.append(weights)
-        moved += groups * weights.size * weights.dtype.itemsize
+        moved += copies * weights.size * weights.dtype.itemsize
     outs = pl.pallas_call(
-        functools.partial(exchange_kernel, count, spread, extra),
+        functools.partial(exchange_kernel, count, spread, spreads, swaps),
         out_shape=tuple(out_shape),
         in_specs=[pl.BlockSpec(memory_space=pl.ANY)] * len(operands),
         out_specs=tuple(pl.BlockSpec(memory_space=pl.ANY) for _ in out_shape),
@@ -137,7 +157,7 @@
 
 
 def gather_chip(block, tag, weights=None):
-    outs = exchange(block, False, tag, weights)
+    outs = exchange(block, False, tag, weights, spreads=weights is not None)
     rows = outs[0].reshape(-1, block.shape[1])
     if weights is None:
         return rows
@@ -150,7 +170,7 @@
     summed = jnp.sum(outs[0].astype(jnp.float32), axis=0)
     if weights is None:
         return summed
-    return summed, outs[1].reshape(-1, weights.shape[1])
+    return summed, outs[1]
 
 
 def gather_group(block):
@@ -242,6 +262,7 @@
     value_w = jnp.concatenate([value_lo, value_hi], axis=1)
     ff_cols = w_gate.shape[1]
     own_mlp = jnp.concatenate([w_gate.astype(bf), w_up.astype(bf), w_down.astype(bf).T], axis=1)
+    own_mlp = lax.all_gather(own_mlp, "group", axis=0, tiled=True)
     half_pos = core_rows(positions, chips, rows_dev)
     half_req = core_rows(request_of, chips, rows_dev)
     heads = 2 * q_cols // HD
@@ -280,8 +301,7 @@
     ) / jnp.transpose(total, (1, 0, 2))
     attended = mixed_heads.astype(bf).reshape(-1, heads * HD)
     attn_part = dot_t(attended, out_w_t)
-    attn_sum, own_mlp = scatter_chip(attn_part.astype(bf), 1, own_mlp)
-    other_mlp = swap_cores(own_mlp)
+    attn_sum, other_mlp = scatter_chip(attn_part.astype(bf), 1, own_mlp)
     mixed = residual + attn_sum
     normed_mlp = gather_chip(rms_scale(mixed, mlp_gain), 2)
     gate_sum = jnp.concatenate(

time: 428 us -> 359 us (0.84)
  Pallas kernels: 309 us -> 247 us
  between operations: 1.74 us -> 15.4 us
  local copies, waits for them, and re-layouts: 23.6 us -> 16.8 us
  starting transfers between devices: 7.06 us -> 2.71 us
    pallas_call x4, Pallas kernels: 309 us -> 247 us  [exchange(): pl.pallas_call(functools.partial(exchange_kernel, count, spread, spreads,...]
    ppermute x1, starting transfers between devices: 6.39 us -> 2.1 us  [from_behind(): return lax.ppermute(block, axis, route)]
  transfers between devices with their start and end apart: 4 -> 4, of which waited for: 1 -> 1; matrix products, arithmetic and copies ran while one was open for 9% -> 13% of each run, Pallas kernels for 13% -> 30%
where the time goes in v2:
time: 359 us; the launch traced here: 354 us
  Pallas kernels  247 us (69%)
  matrix products  38.2 us (11%)
  other arithmetic  25.8 us (7%)
  local copies, waits for them, and re-layouts  16.8 us (5%)
  between operations  15.4 us (4%)
  waiting for transfers between devices  8.38 us (2%)
    pallas_call x4, Pallas kernels, exchange(): pl.pallas_call(functools.partial(exchange_kernel, count, spread, spreads,...  247 us
    dot_general x7, matrix products, dot(): return jnp.dot(acts, weight, preferred_element_type=jnp.float32)  15.7 us
    sub x1, matrix products, body(): probs = jnp.where(visible[None], jnp.exp(scores - row_peak), 0.0)  10.4 us
    ppermute x1, waiting for transfers between devices, from_behind(): return lax.ppermute(block, axis, route)  8.35 us
    dot_general x2, matrix products, dot_t(): lax.dot_general(acts, weight_t, (((1,), (1,)), ((), ())), preferred_eleme...  8.18 us
  transfers between devices with their start and end apart: 4, of which 1 were waited for; matrix products, arithmetic and copies ran while one was open for 13% of the time, Pallas kernels for 30%

profile of v2, /device:TPU:2, one launch (start us, length us, event | category | flops | bytes accessed | tf_op | source)
XLA Modules:
  0.0 354.0 jit_solution(7635590589604589709)
XLA Ops:
  7.3 1.3 copy.60
  8.6 1.1 convert_element_type.114
  9.7 1.1 convert_element_type.115
  14.1 104.9 %shard_map.140 = (bf16[8,96,2048]{2,1,0:T(8,128)(2,1)}, bf16[8,256,384]{2,1,0:T(8,128)(2,1)}) custom-call(bf16[96,2048]{1,0:T(8,128)(2,1)} %fusion.49.refs_0_, bf16[256,384]{1,0:T(8,128)(2,1)} %pad_maximum_fusion.6.refs_1_), custom_call_target="tpu_custom_call" | custom-call | bytes 9437184 | tf_op jit(solution)/shard_map/pallas_call | solution.py:143
  123.0 2.5 multiply_cosine_fusion
  125.6 1.4 compare_and_fusion
  126.9 1.7 pad_add_fusion
  129.2 1.4 copy-done
  130.6 1.3 fusion.37
  132.7 1.2 fusion.38
  136.0 1.1 convolution_convert_fusion.1
  137.8 1.2 broadcast_select_fusion.5
  140.1 1.1 pad_maximum_fusion.1
  141.3 2.1 collective-permute-start.2
  143.4 2.2 subtract_convert_fusion
  145.6 6.1 %scatter_custom_fusion = bf16[8192,128]{1,0:T(8,128)(2,1)} fusion(s32[1536]{0:T(1024)S(1)} %compare_select_fusion, bf16[]{:T(256)} %constant.70.clone.1, bf16[1536,2,128]{2,0,1:T(8,128)(2,1)S(1)} %bitcast.99, s32[]{:T(128)} %constant.58.clone.1, s32[]{:T(128)S(6)} %select_n.66), kind=kCustom, calls=%fused_computation.53 | custom fusion | bytes 2490378 | tf_op jit(solution)/shard_map/scatter | solution.py:333
  151.7 8.4 %collective-permute-done.2 = bf16[512,2,128]{2,0,1:T(8,128)(2,1)} collective-permute-done((bf16[512,2,128]{2,0,1:T(8,128)(2,1)S(1)}, bf16[512,2,128]{2,0,1:T(8,128)(2,1)}, u32[]{:S(2)}, u32[]{:S(2)}) %collective-permute-start.2) | collective-permute-done | bytes 262176 | tf_op jit(solution)/shard_map/ppermute | solution.py:29
  160.1 10.4 %fusion.95 = (f32[2,768]{1,0:T(2,128)S(1)}, bf16[2,768,2048]{1,2,0:T(8,128)(2,1)}) fusion(pred[768,2048]{0,1:T(8,128)(4,1)} %pad_add_fusion, bf16[1536,2,128]{2,0,1:T(8,128)(2,1)S(1)} %bitcast.100, bf16[512,2,128]{2,0,1:T(8,128)(2,1)} %collective-permute-done.2, bf16[768,2,64]{2,0,1:T(8,128)(2,1)} %get-tuple-element.15, ...), kind=kOutput, calls=%fused_computation.135 | convolution fusion | flops 826017792 | bytes 9312256 | tf_op jit(solution)/shard_map/sub | solution.py:297
  170.5 3.9 %fusion.33 = bf16[768,2,128]{0,2,1:T(8,128)(2,1)S(1)} fusion(bf16[2,768,2048]{1,2,0:T(8,128)(2,1)} %get-tuple-element.29, bf16[512,2,128]{2,0,1:T(8,128)(2,1)} %collective-permute-done.2, bf16[1536,2,128]{2,0,1:T(8,128)(2,1)S(1)} %bitcast.101, f32[768,2]{0,1:T(2,128)S(1)} %bitcast.110), kind=kOutput, calls=%fused_computation.35 | convolution fusion | flops 806748160 | bytes 7739392 | tf_op jit(solution)/shard_map/hqk,kd->qhd/dot_general | solution.py:299
  174.4 2.7 convolution_convert_fusion
  177.1 45.6 %shard_map.141 = (bf16[8,96,2048]{2,1,0:T(8,128)(2,1)}, bf16[2048,1536]{1,0:T(8,128)(2,1)}) custom-call(bf16[8,96,2048]{2,1,0:T(8,128)(2,1)} %bitcast.84, bf16[2048,1536]{1,0:T(8,128)(2,1)} %all-gather.2.cloned.1.call-done.refs_1_), custom_call_target="tpu_custom_call" | custom-call | bytes 18874368 | tf_op jit(solution)/shard_map/pallas_call | solution.py:143
  222.8 2.5 convert_reduce_fusion.1
  226.4 49.0 %shard_map.142 = bf16[8,96,2048]{2,1,0:T(8,128)(2,1)} custom-call(bf16[96,2048]{1,0:T(8,128)(2,1)} %multiply_convert_fusion.refs_0_), custom_call_target="tpu_custom_call" | custom-call | bytes 6291456 | tf_op jit(solution)/shard_map/pallas_call | solution.py:143
  275.5 4.5 %fusion.21 = f32[768,512]{0,1:T(8,128)S(1)} fusion(bf16[768,2048]{1,0:T(8,128)(2,1)} %bitcast.90, bf16[2048,1536]{1,0:T(8,128)(2,1)} %get-tuple-element.9), kind=kOutput, calls=%fused_computation.29 | convolution fusion | flops 1610612736 | bytes 6815744 | tf_op jit(solution)/shard_map/dot_general | solution.py:212
  280.0 3.7 %fusion.19 = f32[768,512]{0,1:T(8,128)S(1)} fusion(bf16[768,2048]{1,0:T(8,128)(2,1)S(1)} %bitcast.91, bf16[2048,1536]{1,0:T(8,128)(2,1)} %get-tuple-element.9), kind=kOutput, calls=%fused_computation.27 | convolution fusion | flops 1610612736 | bytes 6815744 | tf_op jit(solution)/shard_map/dot_general | solution.py:212
  283.7 1.7 slice.104
  285.5 1.9 fusion.17
  287.4 1.9 fusion.15
  289.4 1.6 slice-done.2
  290.9 5.5 %fusion.11 = bf16[768,2048]{1,0:T(8,128)(2,1)} fusion(bf16[2048,512]{1,0:T(8,128)(2,1)S(1)} %slice.104, bf16[2048,512]{1,0:T(8,128)(2,1)S(1)} %slice-done.2, f32[768,512]{0,1:T(8,128)S(1)} %fusion.19, f32[768,512]{0,1:T(8,128)S(1)} %fusion.15, f32[768,512]{0,1:T(8,128)S(1)} %fusion.21, f32[768,512]{0,1:T(8,128)S(1)} %fusion.17), kind=kOutput, calls=%fused_computation.18 | convolution fusion | flops 3237478400 | bytes 13631488 | tf_op jit(solution)/shard_map/dot_general | solution.py:216
  296.4 47.3 %shard_map.143 = bf16[8,96,2048]{2,1,0:T(8,128)(2,1)} custom-call(bf16[8,96,2048]{2,1,0:T(8,128)(2,1)} %bitcast.94), custom_call_target="tpu_custom_call" | custom-call | bytes 6291456 | tf_op jit(solution)/shard_map/pallas_call | solution.py:143
  343.7 2.5 convert_reduce_fusion
  (92 shorter events, 13.8 us)
Async XLA Ops:
  7.2 4.6 %copy-start.11 = (f32[256,64]{0,1:T(8,128)S(1)}, f32[256,64]{0,1:T(8,128)}, u32[]{:S(2)}) copy-start(f32[256,64]{0,1:T(8,128)} %param.20) | copy-start | bytes 196612
  7.2 4.7 %copy-start.12 = (f32[256,64]{0,1:T(8,128)S(1)}, f32[256,64]{0,1:T(8,128)}, u32[]{:S(2)}) copy-start(f32[256,64]{0,1:T(8,128)} %param.21) | copy-start | bytes 196612
  7.2 4.9 %copy-start.9 = (f32[128,256]{1,0:T(8,128)S(1)}, f32[128,256]{1,0:T(8,128)}, u32[]{:S(2)}) copy-start(f32[128,256]{1,0:T(8,128)} %param.22) | copy-start | bytes 393220
  7.2 5.0 %copy-start.10 = (f32[256,128]{1,0:T(8,128)S(1)}, f32[256,128]{1,0:T(8,128)}, u32[]{:S(2)}) copy-start(f32[256,128]{1,0:T(8,128)} %param.19) | copy-start | bytes 393220
  7.2 5.8 %copy-start.1 = (bf16[96,2048]{1,0:T(8,128)(2,1)S(1)}, bf16[96,2048]{1,0:T(8,128)(2,1)}, u32[]{:S(2)}) copy-start(bf16[96,2048]{1,0:T(8,128)(2,1)} %param.13) | copy-start | bytes 1179652
  7.2 6.0 %copy-start.13 = (f32[2048]{0:T(1024)S(1)}, f32[2048]{0:T(1024)}, u32[]{:S(2)}) copy-start(f32[2048]{0:T(1024)} %param.17) | copy-start | bytes 24580
  7.2 169.9 %all-gather.2.cloned.1.call-start = ((), (), s32[]{:S(2)}) async-start(), calls=%async_computation | async-start | bytes 7077888 | tf_op jit(solution)/shard_map/all_gather | solution.py:265
  9.7 109.4 %copy-start.8 = (s32[1536]{0:T(1024)S(1)}, s32[1536]{0:T(1024)}, u32[]{:S(2)}) copy-start(s32[1536]{0:T(1024)} %param.14) | copy-start | bytes 18436
  9.7 110.0 %copy-start.7 = (s32[1536]{0:T(1024)S(1)}, s32[1536]{0:T(1024)}, u32[]{:S(2)}) copy-start(s32[1536]{0:T(1024)} %param.15) | copy-start | bytes 18436
  9.7 112.3 %copy-start.15 = (s32[1,64]{1,0:T(1,128)S(1)}, s32[1,64]{1,0:T(1,128)}, u32[]{:S(2)}) copy-start(s32[1,64]{1,0:T(1,128)} %param.16) | copy-start | bytes 772
  119.0 9.8 %collective-permute-start = (bf16[2048,384]{1,0:T(8,128)(2,1)}, bf16[2048,384]{1,0:T(8,128)(2,1)S(1)}, u32[]{:S(2)}, u32[]{:S(2)}) collective-permute-start(bf16[2048,384]{1,0:T(8,128)(2,1)} %bitcast.95), channel_id=1, source_target_pairs={{0,1},{1,0},{2,3},{3,2},{4,5},{5,4},{6,7},{7,6},{8,9},{9,8},{10,11... | collective-permute-start | bytes 4718600 | tf_op jit(solution)/shard_map/ppermute | solution.py:23
  121.0 7.7 %copy-start.3 = (bf16[8,256,384]{2,1,0:T(8,128)(2,1)S(1)}, bf16[8,256,384]{2,1,0:T(8,128)(2,1)}, u32[]{:S(2)}) copy-start(bf16[8,256,384]{2,1,0:T(8,128)(2,1)} %get-tuple-element.7) | copy-start | bytes 4718596
  128.7 1.9 copy-start
  132.7 3.4 copy-start.5
  132.7 3.4 copy-start.6
  134.7 3.0 collective-permute-start.1
  141.3 18.8 %collective-permute-start.2 = (bf16[512,2,128]{2,0,1:T(8,128)(2,1)S(1)}, bf16[512,2,128]{2,0,1:T(8,128)(2,1)}, u32[]{:S(2)}, u32[]{:S(2)}) collective-permute-start(bf16[512,2,128]{2,0,1:T(8,128)(2,1)S(1)} %slice.115), channel_id=1, source_target_pairs={{0,16},{16,32},{32,48},{48,64},{64,80},{80,96},{96,112},{1,17},{17... | collective-permute-start | bytes 786440 | tf_op jit(solution)/shard_map/ppermute | solution.py:29
  170.5 4.0 %copy-start.4 = (bf16[2048,128]{1,0:T(8,128)(2,1)S(1)}, bf16[2048,128]{1,0:T(8,128)(2,1)}, u32[]{:S(2)}) copy-start(bf16[2048,128]{1,0:T(8,128)(2,1)} %get-tuple-element.18) | copy-start | bytes 1572868
  222.8 2.7 copy-start.14
  275.4 4.6 %copy-start.2 = (bf16[8,96,2048]{2,1,0:T(8,128)(2,1)S(1)}, bf16[8,96,2048]{2,1,0:T(8,128)(2,1)}, u32[]{:S(2)}) copy-start(bf16[8,96,2048]{2,1,0:T(8,128)(2,1)} %shard_map.142) | copy-start | bytes 9437188
  275.4 10.0 %slice-start = ((s8[6291456]{0:T(1024)(128)(4,1)}), s8[4194304]{0:T(1024)(128)(4,1)S(1)}, s32[]{:S(2)}) async-start(s8[6291456]{0:T(1024)(128)(4,1)} %bitcast.88), calls=%async_computation.1 | async-start | bytes 8388608
  280.0 5.4 %slice-start.1 = ((s8[6291456]{0:T(1024)(128)(4,1)}), s8[2097152]{0:T(1024)(128)(4,1)S(1)}, s32[]{:S(2)}) async-start(s8[6291456]{0:T(1024)(128)(4,1)} %bitcast.88), calls=%async_computation.2 | async-start | bytes 4194304
  289.4 1.6 slice-start.2
Sparse Core Ops, SparseCore 0:
  11.9 126.7 all-gather.1

commit v3 on v2

--- a/solution.py
+++ b/solution.py
@@ -156,21 +156,20 @@
     return outs
 
 
-def gather_chip(block, tag, weights=None):
-    outs = exchange(block, False, tag, weights, spreads=weights is not None)
-    rows = outs[0].reshape(-1, block.shape[1])
-    if weights is None:
-        return rows
-    return rows, outs[1].reshape(-1, weights.shape[1])
-
-
-def scatter_chip(partial, tag, weights=None):
+def gather_chip(block, tag):
+    outs = exchange(block, False, tag)
+    return outs[0].reshape(-1, block.shape[1])
+
+
+def gather_swap(block, tag, weights):
+    outs = exchange(block, False, tag, weights)
+    return outs[0].reshape(-1, block.shape[1]), outs[1]
+
+
+def scatter_chip(partial, tag):
     count = lax.axis_size("chip")
-    outs = exchange(partial.reshape(count, -1, partial.shape[1]), True, tag, weights)
-    summed = jnp.sum(outs[0].astype(jnp.float32), axis=0)
-    if weights is None:
-        return summed
-    return summed, outs[1]
+    outs = exchange(partial.reshape(count, -1, partial.shape[1]), True, tag)
+    return jnp.sum(outs[0].astype(jnp.float32), axis=0)
 
 
 def gather_group(block):
@@ -247,7 +246,8 @@
     q_cols = wq.shape[1]
     kv_half = wk.shape[1]
     own_attn = jnp.concatenate([wq.astype(bf), wk.astype(bf), wv.astype(bf), wo.astype(bf).T], axis=1)
-    normed, own_attn = gather_chip(rms_scale(residual, attn_gain), 0, own_attn)
+    own_attn = lax.all_gather(own_attn, "group", axis=0, tiled=True)
+    normed = gather_chip(rms_scale(residual, attn_gain), 0)
     other_attn = swap_cores(own_attn)
     query_w = jnp.concatenate([own_attn[:, :q_cols], other_attn[:, :q_cols]], axis=1)
     out_w_t = jnp.concatenate(
@@ -301,9 +301,9 @@
     ) / jnp.transpose(total, (1, 0, 2))
     attended = mixed_heads.astype(bf).reshape(-1, heads * HD)
     attn_part = dot_t(attended, out_w_t)
-    attn_sum, other_mlp = scatter_chip(attn_part.astype(bf), 1, own_mlp)
+    attn_sum = scatter_chip(attn_part.astype(bf), 1)
     mixed = residual + attn_sum
-    normed_mlp = gather_chip(rms_scale(mixed, mlp_gain), 2)
+    normed_mlp, other_mlp = gather_swap(rms_scale(mixed, mlp_gain), 2, own_mlp)
     gate_sum = jnp.concatenate(
         [dot(normed_mlp, own_mlp[:, :ff_cols]), dot(normed_mlp, other_mlp[:, :ff_cols])], axis=1
     )

time: 359 us -> 317 us (0.88)
  the two profiles are of different devices: /device:TPU:2 before, /device:TPU:122 now
where the time goes in v3:
time: 317 us
  Pallas kernels  213 us (67%)
  matrix products  37.2 us (12%)
  other arithmetic  27.2 us (9%)
  local copies, waits for them, and re-layouts  15.8 us (5%)
  between operations  15.2 us (5%)
  waiting for transfers between devices  6.37 us (2%)
    pallas_call x4, Pallas kernels, exchange(): pl.pallas_call(functools.partial(exchange_kernel, count, spread, spreads,...  213 us
    dot_general x7, matrix products, dot(): return jnp.dot(acts, weight, preferred_element_type=jnp.float32)  14.7 us
    sub x1, matrix products, body(): probs = jnp.where(visible[None], jnp.exp(scores - row_peak), 0.0)  10.4 us
    dot_general x2, matrix products, dot_t(): lax.dot_general(acts, weight_t, (((1,), (1,)), ((), ())), preferred_eleme...  8.17 us
  transfers between devices with their start and end apart: 5, of which 2 were waited for; matrix products, arithmetic and copies ran while one was open for 17% of the time, Pallas kernels for 36%

profile of v3, /device:TPU:122, one launch (start us, length us, event | category | flops | bytes accessed | tf_op | source)
XLA Modules:
  0.0 316.6 jit_solution(17536484367742738009)
XLA Ops:
  7.3 1.0 convert_bitcast_fusion.1
  8.2 1.0 copy.33
  11.7 1.2 copy.42
  12.8 1.1 convert_element_type.116
  13.9 1.1 convert_element_type.117
  18.3 66.3 %shard_map.140 = bf16[8,96,2048]{2,1,0:T(8,128)(2,1)} custom-call(bf16[96,2048]{1,0:T(8,128)(2,1)} %fusion.49.refs_0_), custom_call_target="tpu_custom_call" | custom-call | bytes 6291456 | tf_op jit(solution)/shard_map/pallas_call | solution.py:143
  87.4 2.5 multiply_cosine_fusion
  89.9 1.4 compare_and_fusion
  91.3 1.7 pad_add_fusion
  93.8 1.2 fusion.37
  95.8 1.2 fusion.38
  98.5 1.0 convolution_convert_fusion.1
  100.1 1.2 broadcast_select_fusion.1
  102.5 1.1 pad_maximum_fusion.1
  103.7 1.3 collective-permute-start.2
  105.0 2.2 subtract_convert_fusion
  107.2 6.1 %scatter_custom_fusion = bf16[8192,128]{1,0:T(8,128)(2,1)} fusion(s32[1536]{0:T(1024)S(1)} %compare_select_fusion, bf16[]{:T(256)} %constant.70.clone.1, bf16[1536,2,128]{2,0,1:T(8,128)(2,1)S(1)} %bitcast.90, s32[]{:T(128)} %constant.58.clone.1, s32[]{:T(128)S(6)} %select_n.66), kind=kCustom, calls=%fused_computation.53 | custom fusion | bytes 2490378 | tf_op jit(solution)/shard_map/scatter | solution.py:333
  113.3 6.0 %collective-permute-done.2 = bf16[512,2,128]{2,0,1:T(8,128)(2,1)} collective-permute-done((bf16[512,2,128]{2,0,1:T(8,128)(2,1)S(1)}, bf16[512,2,128]{2,0,1:T(8,128)(2,1)}, u32[]{:S(2)}, u32[]{:S(2)}) %collective-permute-start.2) | collective-permute-done | bytes 262176 | tf_op jit(solution)/shard_map/ppermute | solution.py:29
  119.3 10.4 %fusion.95 = (f32[2,768]{1,0:T(2,128)S(1)}, bf16[2,768,2048]{1,2,0:T(8,128)(2,1)}) fusion(pred[768,2048]{0,1:T(8,128)(4,1)} %pad_add_fusion, bf16[1536,2,128]{2,0,1:T(8,128)(2,1)S(1)} %bitcast.91, bf16[512,2,128]{2,0,1:T(8,128)(2,1)} %collective-permute-done.2, bf16[768,2,64]{2,0,1:T(8,128)(2,1)} %get-tuple-element.11, ...), kind=kOutput, calls=%fused_computation.135 | convolution fusion | flops 826017792 | bytes 9312256 | tf_op jit(solution)/shard_map/sub | solution.py:297
  129.7 4.0 %fusion.33 = bf16[768,2,128]{0,2,1:T(8,128)(2,1)S(1)} fusion(bf16[2,768,2048]{1,2,0:T(8,128)(2,1)} %get-tuple-element.25, bf16[512,2,128]{2,0,1:T(8,128)(2,1)} %collective-permute-done.2, bf16[1536,2,128]{2,0,1:T(8,128)(2,1)S(1)} %bitcast.92, f32[768,2]{0,1:T(2,128)S(1)} %bitcast.104), kind=kOutput, calls=%fused_computation.35 | convolution fusion | flops 806748160 | bytes 7739392 | tf_op jit(solution)/shard_map/hqk,kd->qhd/dot_general | solution.py:299
  133.7 2.7 convolution_convert_fusion
  136.4 46.2 %shard_map.141 = bf16[8,96,2048]{2,1,0:T(8,128)(2,1)} custom-call(bf16[8,96,2048]{2,1,0:T(8,128)(2,1)} %bitcast.82), custom_call_target="tpu_custom_call" | custom-call | bytes 6291456 | tf_op jit(solution)/shard_map/pallas_call | solution.py:143
  182.7 2.5 convert_reduce_fusion.1
  186.3 47.5 %shard_map.142 = (bf16[8,96,2048]{2,1,0:T(8,128)(2,1)}, bf16[2048,1536]{1,0:T(8,128)(2,1)}) custom-call(bf16[96,2048]{1,0:T(8,128)(2,1)} %multiply_convert_fusion.refs_0_, bf16[2048,1536]{1,0:T(8,128)(2,1)} %all-gather.5.cloned.1.call-done.refs_1_), custom_call_target="tpu_custom_call" | custom-call | bytes 18874368 | tf_op jit(solution)/shard_map/pallas_call | solution.py:143
  233.8 4.5 %fusion.21 = f32[768,512]{0,1:T(8,128)S(1)} fusion(bf16[768,2048]{1,0:T(8,128)(2,1)} %bitcast.100, bf16[2048,1536]{1,0:T(8,128)(2,1)} %get-tuple-element.5), kind=kOutput, calls=%fused_computation.29 | convolution fusion | flops 1610612736 | bytes 6815744 | tf_op jit(solution)/shard_map/dot_general | solution.py:211
  239.1 3.0 fusion.19
  242.3 1.9 fusion.15
  244.2 1.9 fusion.17
  246.1 1.6 slice-done.2
  248.1 5.4 %fusion.11 = bf16[768,2048]{1,0:T(8,128)(2,1)} fusion(bf16[2048,512]{1,0:T(8,128)(2,1)S(1)} %slice.104, bf16[2048,512]{1,0:T(8,128)(2,1)S(1)} %slice-done.2, f32[768,512]{0,1:T(8,128)S(1)} %copy-done.12, f32[768,512]{0,1:T(8,128)S(1)} %fusion.15, f32[768,512]{0,1:T(8,128)S(1)} %fusion.21, f32[768,512]{0,1:T(8,128)S(1)} %fusion.17), kind=kOutput, calls=%fused_computation.18 | convolution fusion | flops 3237478400 | bytes 13631488 | tf_op jit(solution)/shard_map/dot_general | solution.py:215
  253.6 52.7 %shard_map.143 = bf16[8,96,2048]{2,1,0:T(8,128)(2,1)} custom-call(bf16[8,96,2048]{2,1,0:T(8,128)(2,1)} %bitcast.88), custom_call_target="tpu_custom_call" | custom-call | bytes 6291456 | tf_op jit(solution)/shard_map/pallas_call | solution.py:143
  306.3 2.5 convert_reduce_fusion
  (87 shorter events, 16.0 us)
Async XLA Ops:
  7.2 8.8 %copy-start.7 = (s32[1536]{0:T(1024)S(1)}, s32[1536]{0:T(1024)}, u32[]{:S(2)}) copy-start(s32[1536]{0:T(1024)} %param.14) | copy-start | bytes 18436
  7.2 9.4 %copy-start.6 = (s32[1536]{0:T(1024)S(1)}, s32[1536]{0:T(1024)}, u32[]{:S(2)}) copy-start(s32[1536]{0:T(1024)} %param.15) | copy-start | bytes 18436
  7.2 10.1 %copy-start = (bf16[96,2048]{1,0:T(8,128)(2,1)S(1)}, bf16[96,2048]{1,0:T(8,128)(2,1)}, u32[]{:S(2)}) copy-start(bf16[96,2048]{1,0:T(8,128)(2,1)} %param.13) | copy-start | bytes 1179652
  7.2 10.2 %copy-start.8 = (f32[2048]{0:T(1024)S(1)}, f32[2048]{0:T(1024)}, u32[]{:S(2)}) copy-start(f32[2048]{0:T(1024)} %param.17) | copy-start | bytes 24580
  7.2 82.7 %all-gather.3.cloned.1.call-start = ((), (), s32[]{:S(2)}) async-start(), calls=%async_computation | async-start | bytes 1769472 | tf_op jit(solution)/shard_map/all_gather | solution.py:249
  11.6 174.7 %all-gather.5.cloned.1.call-start = ((), (), s32[]{:S(2)}) async-start(), calls=%async_computation.1 | async-start | bytes 7077888 | tf_op jit(solution)/shard_map/all_gather | solution.py:265
  15.9 70.4 %copy-start.10 = (s32[1,64]{1,0:T(1,128)S(1)}, s32[1,64]{1,0:T(1,128)}, u32[]{:S(2)}) copy-start(s32[1,64]{1,0:T(1,128)} %param.16) | copy-start | bytes 772
  89.9 3.2 copy-start.3
  89.9 3.6 %collective-permute-start = (bf16[2048,384]{0,1:T(8,128)(2,1)}, bf16[2048,384]{0,1:T(8,128)(2,1)S(1)}, u32[]{:S(2)}, u32[]{:S(2)}) collective-permute-start(bf16[2048,384]{0,1:T(8,128)(2,1)} %all-gather.3.cloned.1.call-done), channel_id=1, source_target_pairs={{0,1},{1,0},{2,3},{3,2},{4,5},{5,4},{6,7},{7,6},{8,9},{9,8},{10,11... | collective-permute-start | bytes 4718600 | tf_op jit(solution)/shard_map/ppermute | solution.py:23
  91.3 2.5 copy-start.1
  97.0 1.5 copy-start.4
  97.0 3.1 collective-permute-start.1
  103.7 15.6 %collective-permute-start.2 = (bf16[512,2,128]{2,0,1:T(8,128)(2,1)S(1)}, bf16[512,2,128]{2,0,1:T(8,128)(2,1)}, u32[]{:S(2)}, u32[]{:S(2)}) collective-permute-start(bf16[512,2,128]{2,0,1:T(8,128)(2,1)S(1)} %slice.115), channel_id=1, source_target_pairs={{0,16},{16,32},{32,48},{48,64},{64,80},{80,96},{96,112},{1,17},{17... | collective-permute-start | bytes 786440 | tf_op jit(solution)/shard_map/ppermute | solution.py:29
  129.7 4.0 %copy-start.2 = (bf16[2048,128]{0,1:T(8,128)(2,1)S(1)}, bf16[2048,128]{0,1:T(8,128)(2,1)}, u32[]{:S(2)}) copy-start(bf16[2048,128]{0,1:T(8,128)(2,1)} %get-tuple-element.14) | copy-start | bytes 1572868
  182.6 2.7 copy-start.9
  233.8 4.6 %copy-start.5 = (bf16[2048,1536]{1,0:T(8,128)(2,1)S(1)}, bf16[2048,1536]{1,0:T(8,128)(2,1)}, u32[]{:S(2)}) copy-start(bf16[2048,1536]{1,0:T(8,128)(2,1)} %get-tuple-element.5) | copy-start | bytes 18874372
  233.8 5.3 %copy-start.11 = (bf16[8,96,2048]{2,1,0:T(8,128)(2,1)S(1)}, bf16[8,96,2048]{2,1,0:T(8,128)(2,1)}, u32[]{:S(2)}) copy-start(bf16[8,96,2048]{2,1,0:T(8,128)(2,1)} %get-tuple-element.4) | copy-start | bytes 9437188
  233.8 8.4 %slice-start = ((s8[6291456]{0:T(1024)(128)(4,1)}), s8[4194304]{0:T(1024)(128)(4,1)S(1)}, s32[]{:S(2)}) async-start(s8[6291456]{0:T(1024)(128)(4,1)} %bitcast.83), calls=%async_computation.2 | async-start | bytes 8388608
  239.1 3.2 %slice-start.1 = ((s8[6291456]{0:T(1024)(128)(4,1)}), s8[2097152]{0:T(1024)(128)(4,1)S(1)}, s32[]{:S(2)}) async-start(s8[6291456]{0:T(1024)(128)(4,1)} %bitcast.83), calls=%async_computation.3 | async-start | bytes 4194304
  246.1 1.6 slice-start.2
  246.1 2.0 copy-start.12
Sparse Core Ops, SparseCore 0:
  11.7 49.3 all-gather.2
  62.8 76.8 all-gather.4

commit v4 on v3

--- a/solution.py
+++ b/solution.py
@@ -172,6 +172,131 @@
     return jnp.sum(outs[0].astype(jnp.float32), axis=0)
 
 
+def mlp_kernel(count, ff, own_block, weights, rs_out, own_w, other_w, slots, partials, ag_send, ag_recv, rs_send, rs_recv, swap_sems, local_sems):
+    me = lax.axis_index("chip")
+    group = lax.axis_index("group")
+    core = lax.axis_index("core")
+    mesh_ids = pl.DeviceIdType.MESH
+    barrier = pltpu.get_barrier_semaphore()
+    for shift in range(1, count):
+        peer = lax.rem(me + shift, count)
+        pl.semaphore_signal(barrier, inc=1, device_id=(group, peer, core), device_id_type=mesh_ids)
+    pl.semaphore_signal(barrier, inc=1, device_id=(group, me, 1 - core), device_id_type=mesh_ids)
+    pl.semaphore_wait(barrier, count)
+    load_w = pltpu.make_async_copy(weights, own_w, local_sems.at[0])
+    load_w.start()
+    load_x = pltpu.make_async_copy(own_block, slots.at[me], local_sems.at[1])
+    load_x.start()
+    swap = pltpu.make_async_remote_copy(
+        src_ref=weights,
+        dst_ref=other_w,
+        send_sem=swap_sems.at[0],
+        recv_sem=swap_sems.at[1],
+        device_id=(group, me, 1 - core),
+        device_id_type=mesh_ids,
+    )
+    swap.start()
+    sends = [swap]
+    for shift in range(1, count):
+        peer = lax.rem(me + shift, count)
+        copy = pltpu.make_async_remote_copy(
+            src_ref=own_block,
+            dst_ref=slots.at[me],
+            send_sem=ag_send.at[shift],
+            recv_sem=ag_recv.at[shift],
+            device_id=(group, peer, core),
+            device_id_type=mesh_ids,
+        )
+        copy.start()
+        sends.append(copy)
+    load_w.wait()
+    swap.wait_recv()
+    load_x.wait()
+    outs = []
+    for shift in range(count):
+        sender = lax.rem(me + count - shift, count)
+        if shift > 0:
+            pltpu.make_async_remote_copy(
+                src_ref=slots.at[sender],
+                dst_ref=slots.at[sender],
+                send_sem=ag_send.at[shift],
+                recv_sem=ag_recv.at[shift],
+                device_id=(group, sender, core),
+                device_id_type=mesh_ids,
+            ).wait_recv()
+        rows = slots[sender]
+        total = None
+        for table in (own_w, other_w):
+            gate = jnp.dot(rows, table[:, pl.ds(0, ff)], preferred_element_type=jnp.float32)
+            up = jnp.dot(rows, table[:, pl.ds(ff, ff)], preferred_element_type=jnp.float32)
+            act = (gate / (1.0 + jnp.exp(-gate)) * up).astype(jnp.bfloat16)
+            down = lax.dot_general(
+                act, table[:, pl.ds(2 * ff, ff)], (((1,), (1,)), ((), ())),
+                preferred_element_type=jnp.float32,
+            )
+            total = down if total is None else total + down
+        partials[shift] = total.astype(jnp.bfloat16)
+        if shift == 0:
+            back = pltpu.make_async_copy(partials.at[0], rs_out.at[me], local_sems.at[2])
+        else:
+            back = pltpu.make_async_remote_copy(
+                src_ref=partials.at[shift],
+                dst_ref=rs_out.at[me],
+                send_sem=rs_send.at[shift],
+                recv_sem=rs_recv.at[shift],
+                device_id=(group, sender, core),
+                device_id_type=mesh_ids,
+            )
+        back.start()
+        outs.append(back)
+    for shift in range(1, count):
+        owner = lax.rem(me + shift, count)
+        pltpu.make_async_remote_copy(
+            src_ref=partials.at[shift],
+            dst_ref=rs_out.at[owner],
+            send_sem=rs_send.at[shift],
+            recv_sem=rs_recv.at[shift],
+            device_id=(group, owner, core),
+            device_id_type=mesh_ids,
+        ).wait_recv()
+    outs[0].wait()
+    for copy in outs[1:]:
+        copy.wait_send()
+    for copy in sends:
+        copy.wait_send()
+
+
+def fused_mlp(block, weights, tag):
+    count = lax.axis_size("chip")
+    rows, cols = block.shape
+    ff = weights.shape[1] // 3
+    flops = 2 * count * rows * cols * ff * 6
+    return pl.pallas_call(
+        functools.partial(mlp_kernel, count, ff),
+        out_shape=jax.ShapeDtypeStruct((count, rows, cols), block.dtype),
+        in_specs=[pl.BlockSpec(memory_space=pl.ANY)] * 2,
+        out_specs=pl.BlockSpec(memory_space=pl.ANY),
+        scratch_shapes=[
+            pltpu.VMEM(weights.shape, weights.dtype),
+            pltpu.VMEM(weights.shape, weights.dtype),
+            pltpu.VMEM((count, rows, cols), block.dtype),
+            pltpu.VMEM((count, rows, cols), block.dtype),
+            pltpu.SemaphoreType.DMA((count,)),
+            pltpu.SemaphoreType.DMA((count,)),
+            pltpu.SemaphoreType.DMA((count,)),
+            pltpu.SemaphoreType.DMA((count,)),
+            pltpu.SemaphoreType.DMA((2,)),
+            pltpu.SemaphoreType.DMA((3,)),
+        ],
+        compiler_params=pltpu.CompilerParams(
+            collective_id=tag, has_side_effects=True, vmem_limit_bytes=60 * 1024 * 1024
+        ),
+        cost_estimate=pl.CostEstimate(
+            flops=flops, bytes_accessed=4 * count * rows * cols * 2, transcendentals=count * rows * ff * 2
+        ),
+    )(block, weights)
+
+
 def gather_group(block):
     count = lax.axis_size("group")
     pieces = [block]
@@ -303,21 +428,8 @@
     attn_part = dot_t(attended, out_w_t)
     attn_sum = scatter_chip(attn_part.astype(bf), 1)
     mixed = residual + attn_sum
-    normed_mlp, other_mlp = gather_swap(rms_scale(mixed, mlp_gain), 2, own_mlp)
-    gate_sum = jnp.concatenate(
-        [dot(normed_mlp, own_mlp[:, :ff_cols]), dot(normed_mlp, other_mlp[:, :ff_cols])], axis=1
-    )
-    up_sum = jnp.concatenate(
-        [
-            dot(normed_mlp, own_mlp[:, ff_cols : 2 * ff_cols]),
-            dot(normed_mlp, other_mlp[:, ff_cols : 2 * ff_cols]),
-        ],
-        axis=1,
-    )
-    activation = (jax.nn.silu(gate_sum) * up_sum).astype(bf)
-    down_w_t = jnp.concatenate([own_mlp[:, 2 * ff_cols :], other_mlp[:, 2 * ff_cols :]], axis=1)
-    down_part = dot_t(activation, down_w_t)
-    layer_out = (mixed + scatter_chip(down_part.astype(bf), 3)).astype(bf)
+    partials = fused_mlp(rms_scale(mixed, mlp_gain), own_mlp, 2)
+    layer_out = (mixed + jnp.sum(partials.astype(jnp.float32), axis=0)).astype(bf)
     pages = page_table.shape[1]
     changed = jnp.concatenate(
         [jnp.ones((1,), jnp.int32), (request_of[1:] != request_of[:-1]).astype(jnp.int32)]

time: 317 us -> 300 us (0.946)
  the two profiles are of different devices: /device:TPU:122 before, /device:TPU:2 now
where the time goes in v4:
time: 300 us; the launch traced here: 294 us
  Pallas kernels  202 us (67%)
  other arithmetic  27.1 us (9%)
  matrix products  20.5 us (7%)
  between operations  14.9 us (5%)
  waiting for transfers between devices  13.4 us (4%)
  local copies, waits for them, and re-layouts  12.9 us (4%)
    pallas_call x2, Pallas kernels, exchange(): pl.pallas_call(functools.partial(exchange_kernel, count, spread, spreads,...  106 us
    pallas_call x1, Pallas kernels, fused_mlp(): pl.pallas_call(functools.partial(mlp_kernel, count, ff), out_shape=jax.Sh...  96.4 us
    ppermute x1, waiting for transfers between devices, from_behind(): return lax.ppermute(block, axis, route)  13 us
    sub x1, matrix products, body(): probs = jnp.where(visible[None], jnp.exp(scores - row_peak), 0.0)  10.4 us
    scatter x1, local copies, waits for them, and re-layouts, body(): jnp.zeros((pages * PAGE, width), jnp.bfloat16).at[target].set(own_slice)  6.12 us
  transfers between devices with their start and end apart: 5, of which 2 were waited for; matrix products, arithmetic and copies ran while one was open for 18% of the time, Pallas kernels for 36%

profile of v4, /device:TPU:2, one launch (start us, length us, event | category | flops | bytes accessed | tf_op | source)
XLA Modules:
  0.0 293.6 jit_solution(6453173372106340262)
XLA Ops:
  7.3 1.0 convert_bitcast_fusion.1
  8.2 1.0 copy.33
  9.2 0.8 convert_element_type.94
  11.7 1.2 copy.42
  12.9 1.1 convert_element_type.110
  13.9 1.1 convert_element_type.111
  15.0 0.9 pad_maximum_fusion.1
  17.3 0.9 fusion.31.refs_0_
  18.2 57.2 %shard_map.140 = bf16[8,96,2048]{2,1,0:T(8,128)(2,1)} custom-call(bf16[96,2048]{1,0:T(8,128)(2,1)} %fusion.31.refs_0_), custom_call_target="tpu_custom_call" | custom-call | bytes 6291456 | tf_op jit(solution)/shard_map/pallas_call | solution.py:143
  78.0 2.5 multiply_cosine_fusion
  80.6 1.4 compare_and_fusion
  82.0 1.7 pad_add_fusion
  84.4 1.2 fusion.19
  86.4 1.2 fusion.20
  88.3 0.9 fusion.72
  89.1 1.0 convolution_convert_fusion.1
  90.8 1.2 broadcast_select_fusion.1
  92.0 0.9 copy.35
  93.1 1.1 pad_maximum_fusion
  94.3 1.9 collective-permute-start.2
  96.3 2.2 subtract_convert_fusion
  98.5 6.1 %scatter_custom_fusion = bf16[8192,128]{1,0:T(8,128)(2,1)} fusion(s32[1536]{0:T(1024)S(1)} %compare_select_fusion, bf16[]{:T(256)} %constant.67.clone.1, bf16[1536,2,128]{2,0,1:T(8,128)(2,1)S(1)} %bitcast.81, s32[]{:T(128)} %constant.56.clone.1, s32[]{:T(128)S(6)} %select_n.66), kind=kCustom, calls=%fused_computation.36 | custom fusion | bytes 2490378 | tf_op jit(solution)/shard_map/scatter | solution.py:445
  104.6 13.0 %collective-permute-done.2 = bf16[512,2,128]{2,0,1:T(8,128)(2,1)} collective-permute-done((bf16[512,2,128]{2,0,1:T(8,128)(2,1)S(1)}, bf16[512,2,128]{2,0,1:T(8,128)(2,1)}, u32[]{:S(2)}, u32[]{:S(2)}) %collective-permute-start.2) | collective-permute-done | bytes 262176 | tf_op jit(solution)/shard_map/ppermute | solution.py:29
  117.6 10.4 %fusion.74 = (f32[2,768]{1,0:T(2,128)S(1)}, bf16[2,768,2048]{1,2,0:T(8,128)(2,1)}) fusion(pred[768,2048]{0,1:T(8,128)(4,1)} %pad_add_fusion, bf16[1536,2,128]{2,0,1:T(8,128)(2,1)S(1)} %bitcast.82, bf16[512,2,128]{2,0,1:T(8,128)(2,1)} %collective-permute-done.2, bf16[768,2,64]{2,0,1:T(8,128)(2,1)} %get-tuple-element.7, bf16[768,2,64]{2,0,1:T(8,128)(2,1)} %get-tuple-element.6), kind=kOutput, calls=%fused_computation.115 | convolution fusion | flops 826017792 | bytes 9312256 | tf_op jit(solution)/shard_map/sub | solution.py:422
  128.0 4.0 %fusion.15 = bf16[768,2,128]{0,2,1:T(8,128)(2,1)S(1)} fusion(bf16[2,768,2048]{1,2,0:T(8,128)(2,1)} %get-tuple-element.21, bf16[512,2,128]{2,0,1:T(8,128)(2,1)} %collective-permute-done.2, bf16[1536,2,128]{2,0,1:T(8,128)(2,1)S(1)} %bitcast.83, f32[768,2]{0,1:T(2,128)S(1)} %bitcast.91), kind=kOutput, calls=%fused_computation.18 | convolution fusion | flops 806748160 | bytes 7739392 | tf_op jit(solution)/shard_map/hqk,kd->qhd/dot_general | solution.py:424
  132.0 2.7 convolution_convert_fusion
  134.7 48.6 %shard_map.141 = bf16[8,96,2048]{2,1,0:T(8,128)(2,1)} custom-call(bf16[8,96,2048]{2,1,0:T(8,128)(2,1)} %bitcast.76), custom_call_target="tpu_custom_call" | custom-call | bytes 6291456 | tf_op jit(solution)/shard_map/pallas_call | solution.py:143
  183.3 2.5 convert_reduce_fusion.1
  186.1 0.9 multiply_convert_fusion.own_block
  187.0 96.4 %shard_map.142 = bf16[8,96,2048]{2,1,0:T(8,128)(2,1)} custom-call(bf16[96,2048]{1,0:T(8,128)(2,1)} %multiply_convert_fusion.own_block, bf16[2048,1536]{1,0:T(8,128)(2,1)} %all-gather.5.cloned.1.call-done.weights), custom_call_target="tpu_custom_call" | custom-call | flops 9663676416 | bytes 12582912 | tf_op jit(solution)/shard_map/pallas_call | solution.py:274
  283.3 2.5 convert_reduce_fusion
  285.9 0.9 add_convert_fusion
  (67 shorter events, 8.3 us)
Async XLA Ops:
  7.2 8.8 %copy-start.6 = (s32[1536]{0:T(1024)S(1)}, s32[1536]{0:T(1024)}, u32[]{:S(2)}) copy-start(s32[1536]{0:T(1024)} %param.14) | copy-start | bytes 18436
  7.2 9.4 %copy-start.5 = (s32[1536]{0:T(1024)S(1)}, s32[1536]{0:T(1024)}, u32[]{:S(2)}) copy-start(s32[1536]{0:T(1024)} %param.15) | copy-start | bytes 18436
  7.2 10.0 %copy-start = (bf16[96,2048]{1,0:T(8,128)(2,1)S(1)}, bf16[96,2048]{1,0:T(8,128)(2,1)}, u32[]{:S(2)}) copy-start(bf16[96,2048]{1,0:T(8,128)(2,1)} %param.13) | copy-start | bytes 1179652
  7.2 10.1 %copy-start.7 = (f32[2048]{0:T(1024)S(1)}, f32[2048]{0:T(1024)}, u32[]{:S(2)}) copy-start(f32[2048]{0:T(1024)} %param.17) | copy-start | bytes 24580
  7.2 73.3 %all-gather.3.cloned.1.call-start = ((), (), s32[]{:S(2)}) async-start(), calls=%async_computation | async-start | bytes 1769472 | tf_op jit(solution)/shard_map/all_gather | solution.py:374
  11.6 175.3 %all-gather.5.cloned.1.call-start = ((), (), s32[]{:S(2)}) async-start(), calls=%async_computation.1 | async-start | bytes 7077888 | tf_op jit(solution)/shard_map/all_gather | solution.py:390
  15.9 61.1 %copy-start.9 = (s32[1,64]{1,0:T(1,128)S(1)}, s32[1,64]{1,0:T(1,128)}, u32[]{:S(2)}) copy-start(s32[1,64]{1,0:T(1,128)} %param.16) | copy-start | bytes 772
  80.5 3.2 %copy-start.3 = (bf16[2048,384]{0,1:T(8,128)(2,1)S(1)}, bf16[2048,384]{0,1:T(8,128)(2,1)}, u32[]{:S(2)}) copy-start(bf16[2048,384]{0,1:T(8,128)(2,1)} %all-gather.3.cloned.1.call-done) | copy-start | bytes 4718596
  80.5 3.6 %collective-permute-start = (bf16[2048,384]{0,1:T(8,128)(2,1)}, bf16[2048,384]{0,1:T(8,128)(2,1)S(1)}, u32[]{:S(2)}, u32[]{:S(2)}) collective-permute-start(bf16[2048,384]{0,1:T(8,128)(2,1)} %all-gather.3.cloned.1.call-done), channel_id=1, source_target_pairs={{0,1},{1,0},{2,3},{3,2},{4,5},{5,4},{6,7},{7,6},{8,9},{9,8},{10,11... | collective-permute-start | bytes 4718600 | tf_op jit(solution)/shard_map/ppermute | solution.py:23
  82.0 2.5 copy-start.1
  87.6 2.6 copy-start.4
  87.7 3.1 %collective-permute-start.1 = (bf16[768,2,128]{0,2,1:T(8,128)(2,1)S(1)}, bf16[768,2,128]{0,2,1:T(8,128)(2,1)}, u32[]{:S(2)}, u32[]{:S(2)}) collective-permute-start(bf16[768,2,128]{0,2,1:T(8,128)(2,1)S(1)} %pad_maximum_fusion.3), channel_id=1, source_target_pairs={{0,1},{1,0},{2,3},{3,2},{4,5},{5,4},{6,7},{7,6},{8,9},{9,8},{10,11... | collective-permute-start | bytes 1179656 | tf_op jit(solution)/shard_map/ppermute | solution.py:23
  94.3 23.3 %collective-permute-start.2 = (bf16[512,2,128]{2,0,1:T(8,128)(2,1)S(1)}, bf16[512,2,128]{2,0,1:T(8,128)(2,1)}, u32[]{:S(2)}, u32[]{:S(2)}) collective-permute-start(bf16[512,2,128]{2,0,1:T(8,128)(2,1)S(1)} %slice.91), channel_id=1, source_target_pairs={{0,16},{16,32},{32,48},{48,64},{64,80},{80,96},{96,112},{1,17},{17... | collective-permute-start | bytes 786440 | tf_op jit(solution)/shard_map/ppermute | solution.py:29
  128.0 4.0 %copy-start.2 = (bf16[2048,128]{0,1:T(8,128)(2,1)S(1)}, bf16[2048,128]{0,1:T(8,128)(2,1)}, u32[]{:S(2)}) copy-start(bf16[2048,128]{0,1:T(8,128)(2,1)} %get-tuple-element.10) | copy-start | bytes 1572868
  183.3 2.7 copy-start.8
Sparse Core Ops, SparseCore 0:
  11.7 48.0 all-gather.2
  61.5 84.7 all-gather.4

commit v5 on v4

--- a/solution.py
+++ b/solution.py
@@ -166,13 +166,16 @@
     return outs[0].reshape(-1, block.shape[1]), outs[1]
 
 
-def scatter_chip(partial, tag):
+def scatter_chip(partial, tag, weights=None):
     count = lax.axis_size("chip")
-    outs = exchange(partial.reshape(count, -1, partial.shape[1]), True, tag)
-    return jnp.sum(outs[0].astype(jnp.float32), axis=0)
-
-
-def mlp_kernel(count, ff, own_block, weights, rs_out, own_w, other_w, slots, partials, ag_send, ag_recv, rs_send, rs_recv, swap_sems, local_sems):
+    outs = exchange(partial.reshape(count, -1, partial.shape[1]), True, tag, weights)
+    summed = jnp.sum(outs[0].astype(jnp.float32), axis=0)
+    if weights is None:
+        return summed
+    return summed, outs[1]
+
+
+def mlp_kernel(count, ff, own_block, weights, other_weights, rs_out, own_w, other_w, slots, partials, ag_send, ag_recv, rs_send, rs_recv, swap_sems, local_sems):
     me = lax.axis_index("chip")
     group = lax.axis_index("group")
     core = lax.axis_index("core")
@@ -181,22 +184,14 @@
     for shift in range(1, count):
         peer = lax.rem(me + shift, count)
         pl.semaphore_signal(barrier, inc=1, device_id=(group, peer, core), device_id_type=mesh_ids)
-    pl.semaphore_signal(barrier, inc=1, device_id=(group, me, 1 - core), device_id_type=mesh_ids)
-    pl.semaphore_wait(barrier, count)
+    pl.semaphore_wait(barrier, count - 1)
     load_w = pltpu.make_async_copy(weights, own_w, local_sems.at[0])
     load_w.start()
     load_x = pltpu.make_async_copy(own_block, slots.at[me], local_sems.at[1])
     load_x.start()
-    swap = pltpu.make_async_remote_copy(
-        src_ref=weights,
-        dst_ref=other_w,
-        send_sem=swap_sems.at[0],
-        recv_sem=swap_sems.at[1],
-        device_id=(group, me, 1 - core),
-        device_id_type=mesh_ids,
-    )
-    swap.start()
-    sends = [swap]
+    load_other = pltpu.make_async_copy(other_weights, other_w, swap_sems.at[0])
+    load_other.start()
+    sends = []
     for shift in range(1, count):
         peer = lax.rem(me + shift, count)
         copy = pltpu.make_async_remote_copy(
@@ -210,7 +205,7 @@
         copy.start()
         sends.append(copy)
     load_w.wait()
-    swap.wait_recv()
+    load_other.wait()
     load_x.wait()
     outs = []
     for shift in range(count):
@@ -266,7 +261,7 @@
         copy.wait_send()
 
 
-def fused_mlp(block, weights, tag):
+def fused_mlp(block, weights, other_weights, tag):
     count = lax.axis_size("chip")
     rows, cols = block.shape
     ff = weights.shape[1] // 3
@@ -274,7 +269,7 @@
     return pl.pallas_call(
         functools.partial(mlp_kernel, count, ff),
         out_shape=jax.ShapeDtypeStruct((count, rows, cols), block.dtype),
-        in_specs=[pl.BlockSpec(memory_space=pl.ANY)] * 2,
+        in_specs=[pl.BlockSpec(memory_space=pl.ANY)] * 3,
         out_specs=pl.BlockSpec(memory_space=pl.ANY),
         scratch_shapes=[
             pltpu.VMEM(weights.shape, weights.dtype),
@@ -294,7 +289,7 @@
         cost_estimate=pl.CostEstimate(
             flops=flops, bytes_accessed=4 * count * rows * cols * 2, transcendentals=count * rows * ff * 2
         ),
-    )(block, weights)
+    )(block, weights, other_weights)
 
 
 def gather_group(block):
@@ -426,9 +421,9 @@
     ) / jnp.transpose(total, (1, 0, 2))
     attended = mixed_heads.astype(bf).reshape(-1, heads * HD)
     attn_part = dot_t(attended, out_w_t)
-    attn_sum = scatter_chip(attn_part.astype(bf), 1)
+    attn_sum, other_mlp = scatter_chip(attn_part.astype(bf), 1, own_mlp)
     mixed = residual + attn_sum
-    partials = fused_mlp(rms_scale(mixed, mlp_gain), own_mlp, 2)
+    partials = fused_mlp(rms_scale(mixed, mlp_gain), own_mlp, other_mlp, 2)
     layer_out = (mixed + jnp.sum(partials.astype(jnp.float32), axis=0)).astype(bf)
     pages = page_table.shape[1]
     changed = jnp.concatenate(

time: 300 us -> 303 us (1.010); the launches traced: 294 us -> 303 us
  waiting for transfers between devices: 13.4 us -> 25.4 us
    all_gather x1, waiting for transfers between devices: 0.01 us -> 10.9 us  [body(): own_mlp = lax.all_gather(own_mlp, 'group', axis=0, tiled=True)]
    pallas_call x2, Pallas kernels: 106 us -> 101 us  [exchange(): pl.pallas_call(functools.partial(exchange_kernel, count, spread, spreads,...]
  transfers between devices with their start and end apart: 5 -> 5, of which waited for: 2 -> 3; matrix products, arithmetic and copies ran while one was open for 18% -> 16% of each run, Pallas kernels for 36% -> 19%
where the time goes in v5:
time: 303 us
  Pallas kernels  199 us (66%)
  other arithmetic  27.2 us (9%)
  waiting for transfers between devices  25.4 us (8%)
  matrix products  20.5 us (7%)
  between operations  15 us (5%)
  local copies, waits for them, and re-layouts  12.9 us (4%)
    pallas_call x2, Pallas kernels, exchange(): pl.pallas_call(functools.partial(exchange_kernel, count, spread, spreads,...  101 us
    pallas_call x1, Pallas kernels, fused_mlp(): pl.pallas_call(functools.partial(mlp_kernel, count, ff), out_shape=jax.Sh...  98 us
    ppermute x1, waiting for transfers between devices, from_behind(): return lax.ppermute(block, axis, route)  14.1 us
    all_gather x1, waiting for transfers between devices, body(): own_mlp = lax.all_gather(own_mlp, 'group', axis=0, tiled=True)  10.9 us
    sub x1, matrix products, body(): probs = jnp.where(visible[None], jnp.exp(scores - row_peak), 0.0)  10.4 us
    scatter x1, local copies, waits for them, and re-layouts, body(): jnp.zeros((pages * PAGE, width), jnp.bfloat16).at[target].set(own_slice)  6.12 us
  transfers between devices with their start and end apart: 5, of which 3 were waited for; matrix products, arithmetic and copies ran while one was open for 16% of the time, Pallas kernels for 19%

profile of v5, /device:TPU:2, one launch (start us, length us, event | category | flops | bytes accessed | tf_op | source)
XLA Modules:
  0.0 302.8 jit_solution(12955173408083523298)
XLA Ops:
  7.3 1.0 convert_bitcast_fusion.1
  8.2 1.0 copy.33
  11.7 1.2 copy.42
  12.9 1.1 convert_element_type.108
  13.9 1.1 convert_element_type.109
  15.0 1.0 pad_maximum_fusion.1
  17.4 0.9 fusion.31.refs_0_
  18.4 56.6 %shard_map.140 = bf16[8,96,2048]{2,1,0:T(8,128)(2,1)} custom-call(bf16[96,2048]{1,0:T(8,128)(2,1)} %fusion.31.refs_0_), custom_call_target="tpu_custom_call" | custom-call | bytes 6291456 | tf_op jit(solution)/shard_map/pallas_call | solution.py:143
  77.7 2.5 multiply_cosine_fusion
  80.2 1.4 compare_and_fusion
  81.6 1.7 pad_add_fusion
  84.0 1.2 fusion.19
  86.0 1.2 fusion.20
  87.8 0.9 fusion.72
  88.7 1.0 convolution_convert_fusion.1
  90.4 1.2 broadcast_select_fusion.1
  91.6 0.9 copy.35
  92.7 1.1 pad_maximum_fusion
  93.9 1.9 collective-permute-start.2
  95.9 2.2 subtract_convert_fusion
  98.1 6.1 %scatter_custom_fusion = bf16[8192,128]{1,0:T(8,128)(2,1)} fusion(s32[1536]{0:T(1024)S(1)} %compare_select_fusion, bf16[]{:T(256)} %constant.67.clone.1, bf16[1536,2,128]{2,0,1:T(8,128)(2,1)S(1)} %bitcast.81, s32[]{:T(128)} %constant.56.clone.1, s32[]{:T(128)S(6)} %select_n.66), kind=kCustom, calls=%fused_computation.36 | custom fusion | bytes 2490378 | tf_op jit(solution)/shard_map/scatter | solution.py:440
  104.2 14.1 %collective-permute-done.2 = bf16[512,2,128]{2,0,1:T(8,128)(2,1)} collective-permute-done((bf16[512,2,128]{2,0,1:T(8,128)(2,1)S(1)}, bf16[512,2,128]{2,0,1:T(8,128)(2,1)}, u32[]{:S(2)}, u32[]{:S(2)}) %collective-permute-start.2) | collective-permute-done | bytes 262176 | tf_op jit(solution)/shard_map/ppermute | solution.py:29
  118.3 10.4 %fusion.74 = (f32[2,768]{1,0:T(2,128)S(1)}, bf16[2,768,2048]{1,2,0:T(8,128)(2,1)}) fusion(pred[768,2048]{0,1:T(8,128)(4,1)} %pad_add_fusion, bf16[1536,2,128]{2,0,1:T(8,128)(2,1)S(1)} %bitcast.82, bf16[512,2,128]{2,0,1:T(8,128)(2,1)} %collective-permute-done.2, bf16[768,2,64]{2,0,1:T(8,128)(2,1)} %get-tuple-element.11, ...), kind=kOutput, calls=%fused_computation.115 | convolution fusion | flops 826017792 | bytes 9312256 | tf_op jit(solution)/shard_map/sub | solution.py:417
  128.7 4.0 %fusion.15 = bf16[768,2,128]{0,2,1:T(8,128)(2,1)S(1)} fusion(bf16[2,768,2048]{1,2,0:T(8,128)(2,1)} %get-tuple-element.25, bf16[512,2,128]{2,0,1:T(8,128)(2,1)} %collective-permute-done.2, bf16[1536,2,128]{2,0,1:T(8,128)(2,1)S(1)} %bitcast.83, f32[768,2]{0,1:T(2,128)S(1)} %bitcast.91), kind=kOutput, calls=%fused_computation.18 | convolution fusion | flops 806748160 | bytes 7739392 | tf_op jit(solution)/shard_map/hqk,kd->qhd/dot_general | solution.py:419
  132.8 2.7 convolution_convert_fusion
  135.4 10.9 %all-gather.5.cloned.1.call-done.refs_1_.weights = bf16[2048,1536]{1,0:T(8,128)(2,1)} async-done(((bf16[256,1536]{1,0:T(8,128)(2,1)}), bf16[2048,1536]{1,0:T(8,128)(2,1)}) %all-gather.5.cloned.1.call-update) | async-done | bytes 6291472 | tf_op jit(solution)/shard_map/all_gather | solution.py:385
  146.3 44.5 %shard_map.141 = (bf16[8,96,2048]{2,1,0:T(8,128)(2,1)}, bf16[2048,1536]{1,0:T(8,128)(2,1)}) custom-call(bf16[8,96,2048]{2,1,0:T(8,128)(2,1)} %bitcast.76, bf16[2048,1536]{1,0:T(8,128)(2,1)} %all-gather.5.cloned.1.call-done.refs_1_.weights), custom_call_target="tpu_custom_call" | custom-call | bytes 18874368 | tf_op jit(solution)/shard_map/pallas_call | solution.py:143
  190.9 2.5 convert_reduce_fusion.1
  193.6 0.9 multiply_convert_fusion.own_block
  194.5 98.0 %shard_map.142 = bf16[8,96,2048]{2,1,0:T(8,128)(2,1)} custom-call(bf16[96,2048]{1,0:T(8,128)(2,1)} %multiply_convert_fusion.own_block, bf16[2048,1536]{1,0:T(8,128)(2,1)} %all-gather.5.cloned.1.call-done.refs_1_.weights, bf16[2048,1536]{1,0:T(8,128)(2,1)} %get-tuple-element.5.other_weights), custom_call_target="tpu_custom_call" | custom-call | flops 9663676416 | bytes 12582912 | tf_op jit(solution)/shard_map/pallas_call | solution.py:269
  292.5 2.5 convert_reduce_fusion
  295.1 0.9 add_convert_fusion
  (67 shorter events, 9.2 us)
Async XLA Ops:
  7.2 8.8 %copy-start.6 = (s32[1536]{0:T(1024)S(1)}, s32[1536]{0:T(1024)}, u32[]{:S(2)}) copy-start(s32[1536]{0:T(1024)} %param.14) | copy-start | bytes 18436
  7.2 9.4 %copy-start.5 = (s32[1536]{0:T(1024)S(1)}, s32[1536]{0:T(1024)}, u32[]{:S(2)}) copy-start(s32[1536]{0:T(1024)} %param.15) | copy-start | bytes 18436
  7.2 10.1 %copy-start = (bf16[96,2048]{1,0:T(8,128)(2,1)S(1)}, bf16[96,2048]{1,0:T(8,128)(2,1)}, u32[]{:S(2)}) copy-start(bf16[96,2048]{1,0:T(8,128)(2,1)} %param.13) | copy-start | bytes 1179652
  7.2 10.2 %copy-start.7 = (f32[2048]{0:T(1024)S(1)}, f32[2048]{0:T(1024)}, u32[]{:S(2)}) copy-start(f32[2048]{0:T(1024)} %param.17) | copy-start | bytes 24580
  7.2 72.9 %all-gather.3.cloned.1.call-start = ((), (), s32[]{:S(2)}) async-start(), calls=%async_computation | async-start | bytes 1769472 | tf_op jit(solution)/shard_map/all_gather | solution.py:369
  11.6 134.7 %all-gather.5.cloned.1.call-start = ((), (), s32[]{:S(2)}) async-start(), calls=%async_computation.1 | async-start | bytes 7077888 | tf_op jit(solution)/shard_map/all_gather | solution.py:385
  16.0 60.6 %copy-start.9 = (s32[1,64]{1,0:T(1,128)S(1)}, s32[1,64]{1,0:T(1,128)}, u32[]{:S(2)}) copy-start(s32[1,64]{1,0:T(1,128)} %param.16) | copy-start | bytes 772
  80.1 3.2 %copy-start.3 = (bf16[2048,384]{0,1:T(8,128)(2,1)S(1)}, bf16[2048,384]{0,1:T(8,128)(2,1)}, u32[]{:S(2)}) copy-start(bf16[2048,384]{0,1:T(8,128)(2,1)} %all-gather.3.cloned.1.call-done) | copy-start | bytes 4718596
  80.1 3.6 %collective-permute-start = (bf16[2048,384]{0,1:T(8,128)(2,1)}, bf16[2048,384]{0,1:T(8,128)(2,1)S(1)}, u32[]{:S(2)}, u32[]{:S(2)}) collective-permute-start(bf16[2048,384]{0,1:T(8,128)(2,1)} %all-gather.3.cloned.1.call-done), channel_id=1, source_target_pairs={{0,1},{1,0},{2,3},{3,2},{4,5},{5,4},{6,7},{7,6},{8,9},{9,8},{10,11... | collective-permute-start | bytes 4718600 | tf_op jit(solution)/shard_map/ppermute | solution.py:23
  81.5 2.5 copy-start.1
  87.2 2.5 copy-start.4
  87.3 3.1 %collective-permute-start.1 = (bf16[768,2,128]{0,2,1:T(8,128)(2,1)S(1)}, bf16[768,2,128]{0,2,1:T(8,128)(2,1)}, u32[]{:S(2)}, u32[]{:S(2)}) collective-permute-start(bf16[768,2,128]{0,2,1:T(8,128)(2,1)S(1)} %pad_maximum_fusion.3), channel_id=1, source_target_pairs={{0,1},{1,0},{2,3},{3,2},{4,5},{5,4},{6,7},{7,6},{8,9},{9,8},{10,11... | collective-permute-start | bytes 1179656 | tf_op jit(solution)/shard_map/ppermute | solution.py:23
  93.9 24.4 %collective-permute-start.2 = (bf16[512,2,128]{2,0,1:T(8,128)(2,1)S(1)}, bf16[512,2,128]{2,0,1:T(8,128)(2,1)}, u32[]{:S(2)}, u32[]{:S(2)}) collective-permute-start(bf16[512,2,128]{2,0,1:T(8,128)(2,1)S(1)} %slice.91), channel_id=1, source_target_pairs={{0,16},{16,32},{32,48},{48,64},{64,80},{80,96},{96,112},{1,17},{17... | collective-permute-start | bytes 786440 | tf_op jit(solution)/shard_map/ppermute | solution.py:29
  128.7 4.0 %copy-start.2 = (bf16[2048,128]{0,1:T(8,128)(2,1)S(1)}, bf16[2048,128]{0,1:T(8,128)(2,1)}, u32[]{:S(2)}) copy-start(bf16[2048,128]{0,1:T(8,128)(2,1)} %get-tuple-element.14) | copy-start | bytes 1572868
  190.9 2.7 copy-start.8
Sparse Core Ops, SparseCore 0:
  11.7 48.0 all-gather.2
  61.5 84.7 all-gather.4

commit v6 on v4

--- a/solution.py
+++ b/solution.py
@@ -442,7 +442,11 @@
     target = chosen * PAGE + positions % PAGE
     own_slice = lax.dynamic_index_in_dim(kv_rows, lax.axis_index("core"), axis=1, keepdims=False)
     width = own_slice.shape[1]
-    cache = jnp.zeros((pages * PAGE, width), jnp.bfloat16).at[target].set(own_slice)
+    source_row = jnp.full((pages * PAGE,), tok_group, jnp.int32).at[target].set(
+        jnp.arange(tok_group, dtype=jnp.int32)
+    )
+    padded = jnp.concatenate([own_slice, jnp.zeros((1, width), own_slice.dtype)], axis=0)
+    cache = jnp.take(padded, source_row, axis=0)
     return (layer_out, cache.reshape(pages, PAGE, width))
 
 

time: 300 us -> 324 us (1.080); the launches traced: 294 us -> 321 us
  local copies, waits for them, and re-layouts: 12.9 us -> 40.9 us
  waiting for transfers between devices: 13.4 us -> 0.06 us
  Pallas kernels: 202 us -> 214 us
    gather x0 -> x1, local copies, waits for them, and re-layouts: none -> 27.9 us  [body(): cache = jnp.take(padded, source_row, axis=0)]
    ppermute x1, waiting for transfers between devices: 13 us -> 0.01 us  [from_behind(): return lax.ppermute(block, axis, route)]
    pallas_call x1, Pallas kernels: 96.4 us -> 103 us  [fused_mlp(): pl.pallas_call(functools.partial(mlp_kernel, count, ff), out_shape=jax.Sh...]
    pallas_call x2, Pallas kernels: 106 us -> 111 us  [exchange(): pl.pallas_call(functools.partial(exchange_kernel, count, spread, spreads,...]
  transfers between devices with their start and end apart: 5 -> 5, of which waited for: 2 -> 0; matrix products, arithmetic and copies ran while one was open for 18% -> 25% of each run, Pallas kernels for 36% -> 34%
where the time goes in v6:
time: 324 us; the launch traced here: 321 us
  Pallas kernels  214 us (66%)
  local copies, waits for them, and re-layouts  40.9 us (13%)
  other arithmetic  27.9 us (9%)
  matrix products  20.5 us (6%)
  between operations  15.1 us (5%)
    pallas_call x2, Pallas kernels, exchange(): pl.pallas_call(functools.partial(exchange_kernel, count, spread, spreads,...  111 us
    pallas_call x1, Pallas kernels, fused_mlp(): pl.pallas_call(functools.partial(mlp_kernel, count, ff), out_shape=jax.Sh...  103 us
    gather x1, local copies, waits for them, and re-layouts, body(): cache = jnp.take(padded, source_row, axis=0)  27.9 us
    sub x1, matrix products, body(): probs = jnp.where(visible[None], jnp.exp(scores - row_peak), 0.0)  10.4 us
  transfers between devices with their start and end apart: 5, of which 0 were waited for; matrix products, arithmetic and copies ran while one was open for 25% of the time, Pallas kernels for 34%

profile of v6, /device:TPU:2, one launch (start us, length us, event | category | flops | bytes accessed | tf_op | source)
XLA Modules:
  0.0 321.1 jit_solution(340624138483620045)
XLA Ops:
  7.3 1.0 convert_bitcast_fusion.1
  8.2 1.0 copy.33
  9.3 0.8 convert_element_type.94
  11.7 1.2 copy.42
  12.9 1.1 convert_element_type.110
  14.0 1.1 convert_element_type.111
  15.1 0.9 pad_maximum_fusion.1
  17.4 0.9 fusion.29.refs_0_
  18.3 57.2 %shard_map.140 = bf16[8,96,2048]{2,1,0:T(8,128)(2,1)} custom-call(bf16[96,2048]{1,0:T(8,128)(2,1)} %fusion.29.refs_0_), custom_call_target="tpu_custom_call" | custom-call | bytes 6291456 | tf_op jit(solution)/shard_map/pallas_call | solution.py:143
  77.2 6.2 %scatter_custom_fusion = s32[8192]{0:T(1024)S(1)} fusion(s32[1536]{0:T(1024)S(1)} %compare_select_fusion.1, s32[1536]{0:T(1024)S(1)} %iota.22, s32[]{:T(128)} %constant.80.clone.1), kind=kCustom, calls=%fused_computation.90 | custom fusion | bytes 32772 | tf_op jit(solution)/shard_map/scatter | solution.py:445
  84.9 1.4 multiply_cosine_fusion
  86.5 1.4 compare_and_fusion
  87.9 1.7 pad_add_fusion
  89.6 0.9 fusion.70
  90.6 1.2 fusion.19
  92.6 1.2 fusion.20
  95.0 0.9 fusion.71
  96.0 1.0 convolution_convert_fusion.1
  97.6 1.1 subtract_convert_fusion
  98.7 1.1 broadcast_select_fusion.2
  100.5 2.1 collective-permute-start.2
  102.7 27.9 %gather_fusion = bf16[8192,128]{1,0:T(8,128)(2,1)S(1)} fusion(bf16[1537,128]{1,0:T(8,128)(2,1)S(1)} %concatenate.61, s32[8192]{0:T(1024)} %fusion.55), kind=kCustom, calls=%fused_computation | custom fusion | bytes 4227072 | tf_op jit(solution)/shard_map/jit(_take)/gather | solution.py:449
  130.7 2.6 broadcast_select_fusion
  133.3 10.4 %fusion.73 = (f32[2,768]{1,0:T(2,128)S(1)}, bf16[2,768,2048]{1,2,0:T(8,128)(2,1)}) fusion(pred[768,2048]{0,1:T(8,128)(4,1)} %pad_add_fusion, bf16[1536,2,128]{2,0,1:T(8,128)(2,1)S(1)} %bitcast.84, bf16[512,2,128]{2,0,1:T(8,128)(2,1)} %collective-permute-done.2, bf16[768,2,64]{2,0,1:T(8,128)(2,1)} %get-tuple-element.7, bf16[768,2,64]{2,0,1:T(8,128)(2,1)} %get-tuple-element.6), kind=kOutput, calls=%fused_computation.119 | convolution fusion | flops 826017792 | bytes 9312256 | tf_op jit(solution)/shard_map/sub | solution.py:422
  143.8 4.0 %fusion.15 = bf16[768,2,128]{0,2,1:T(8,128)(2,1)S(1)} fusion(bf16[2,768,2048]{1,2,0:T(8,128)(2,1)} %get-tuple-element.21, bf16[512,2,128]{2,0,1:T(8,128)(2,1)} %collective-permute-done.2, bf16[1536,2,128]{2,0,1:T(8,128)(2,1)S(1)} %bitcast.85, f32[768,2]{0,1:T(2,128)S(1)} %bitcast.92), kind=kOutput, calls=%fused_computation.20 | convolution fusion | flops 806748160 | bytes 7739392 | tf_op jit(solution)/shard_map/hqk,kd->qhd/dot_general | solution.py:424
  147.8 2.7 convolution_convert_fusion
  150.5 53.4 %shard_map.141 = bf16[8,96,2048]{2,1,0:T(8,128)(2,1)} custom-call(bf16[8,96,2048]{2,1,0:T(8,128)(2,1)} %bitcast.77), custom_call_target="tpu_custom_call" | custom-call | bytes 6291456 | tf_op jit(solution)/shard_map/pallas_call | solution.py:143
  203.9 2.5 convert_reduce_fusion.1
  206.6 0.9 multiply_convert_fusion.own_block
  207.5 103.3 %shard_map.142 = bf16[8,96,2048]{2,1,0:T(8,128)(2,1)} custom-call(bf16[96,2048]{1,0:T(8,128)(2,1)} %multiply_convert_fusion.own_block, bf16[2048,1536]{1,0:T(8,128)(2,1)} %all-gather.5.cloned.1.call-done.weights), custom_call_target="tpu_custom_call" | custom-call | flops 9663676416 | bytes 12582912 | tf_op jit(solution)/shard_map/pallas_call | solution.py:274
  310.8 2.5 convert_reduce_fusion
  313.4 0.9 add_convert_fusion
  (78 shorter events, 9.3 us)
Async XLA Ops:
  7.2 8.8 %copy-start = (bf16[96,2048]{1,0:T(8,128)(2,1)S(1)}, bf16[96,2048]{1,0:T(8,128)(2,1)}, u32[]{:S(2)}) copy-start(bf16[96,2048]{1,0:T(8,128)(2,1)} %param.13) | copy-start | bytes 1179652
  7.2 9.0 %copy-start.8 = (s32[1536]{0:T(1024)S(1)}, s32[1536]{0:T(1024)}, u32[]{:S(2)}) copy-start(s32[1536]{0:T(1024)} %param.14) | copy-start | bytes 18436
  7.2 9.6 %copy-start.7 = (s32[1536]{0:T(1024)S(1)}, s32[1536]{0:T(1024)}, u32[]{:S(2)}) copy-start(s32[1536]{0:T(1024)} %param.15) | copy-start | bytes 18436
  7.2 10.2 %copy-start.9 = (f32[2048]{0:T(1024)S(1)}, f32[2048]{0:T(1024)}, u32[]{:S(2)}) copy-start(f32[2048]{0:T(1024)} %param.17) | copy-start | bytes 24580
  7.2 79.1 %all-gather.3.cloned.1.call-start = ((), (), s32[]{:S(2)}) async-start(), calls=%async_computation | async-start | bytes 1769472 | tf_op jit(solution)/shard_map/all_gather | solution.py:374
  11.7 195.8 %all-gather.5.cloned.1.call-start = ((), (), s32[]{:S(2)}) async-start(), calls=%async_computation.1 | async-start | bytes 7077888 | tf_op jit(solution)/shard_map/all_gather | solution.py:390
  16.0 61.1 %copy-start.11 = (s32[1,64]{1,0:T(1,128)S(1)}, s32[1,64]{1,0:T(1,128)}, u32[]{:S(2)}) copy-start(s32[1,64]{1,0:T(1,128)} %param.16) | copy-start | bytes 772
  86.4 3.3 %copy-start.6 = (bf16[2048,384]{0,1:T(8,128)(2,1)S(1)}, bf16[2048,384]{0,1:T(8,128)(2,1)}, u32[]{:S(2)}) copy-start(bf16[2048,384]{0,1:T(8,128)(2,1)} %all-gather.3.cloned.1.call-done) | copy-start | bytes 4718596
  86.4 4.1 %collective-permute-start = (bf16[2048,384]{0,1:T(8,128)(2,1)}, bf16[2048,384]{0,1:T(8,128)(2,1)S(1)}, u32[]{:S(2)}, u32[]{:S(2)}) collective-permute-start(bf16[2048,384]{0,1:T(8,128)(2,1)} %all-gather.3.cloned.1.call-done), channel_id=1, source_target_pairs={{0,1},{1,0},{2,3},{3,2},{4,5},{5,4},{6,7},{7,6},{8,9},{9,8},{10,11... | collective-permute-start | bytes 4718600 | tf_op jit(solution)/shard_map/ppermute | solution.py:23
  87.9 2.7 copy-start.1
  94.6 4.2 %collective-permute-start.1 = (bf16[768,2,128]{0,2,1:T(8,128)(2,1)}, bf16[768,2,128]{0,2,1:T(8,128)(2,1)}, u32[]{:S(2)}, u32[]{:S(2)}) collective-permute-start(bf16[768,2,128]{0,2,1:T(8,128)(2,1)} %pad_maximum_fusion.3), channel_id=1, source_target_pairs={{0,1},{1,0},{2,3},{3,2},{4,5},{5,4},{6,7},{7,6},{8,9},{9,8},{10,11... | collective-permute-start | bytes 1179656 | tf_op jit(solution)/shard_map/ppermute | solution.py:23
  100.5 2.2 copy-start.2
  100.5 32.8 %collective-permute-start.2 = (bf16[512,2,128]{2,0,1:T(8,128)(2,1)S(1)}, bf16[512,2,128]{2,0,1:T(8,128)(2,1)}, u32[]{:S(2)}, u32[]{:S(2)}) collective-permute-start(bf16[512,2,128]{2,0,1:T(8,128)(2,1)S(1)} %slice.93), channel_id=1, source_target_pairs={{0,16},{16,32},{32,48},{48,64},{64,80},{80,96},{96,112},{1,17},{17... | collective-permute-start | bytes 786440 | tf_op jit(solution)/shard_map/ppermute | solution.py:29
  130.7 2.6 copy-start.3
  143.7 4.0 %copy-start.4 = (bf16[2048,128]{0,1:T(8,128)(2,1)S(1)}, bf16[2048,128]{0,1:T(8,128)(2,1)}, u32[]{:S(2)}) copy-start(bf16[2048,128]{0,1:T(8,128)(2,1)} %get-tuple-element.8) | copy-start | bytes 1572868
  143.8 4.0 %copy-start.5 = (bf16[2048,128]{0,1:T(8,128)(2,1)S(1)}, bf16[2048,128]{0,1:T(8,128)(2,1)}, u32[]{:S(2)}) copy-start(bf16[2048,128]{0,1:T(8,128)(2,1)} %get-tuple-element.10) | copy-start | bytes 1572868
  203.9 2.7 copy-start.10
Sparse Core Ops, SparseCore 0:
  11.8 48.0 all-gather.2
  61.5 84.4 all-gather.4

commit v7 on v4

--- a/solution.py
+++ b/solution.py
@@ -13,6 +13,7 @@
 HD = 128
 PAGE = 128
 MAXLEN = 512
+SWAP_PARTS = 4
 
 
 rope_base = 1000000.0
@@ -187,16 +188,22 @@
     load_w.start()
     load_x = pltpu.make_async_copy(own_block, slots.at[me], local_sems.at[1])
     load_x.start()
-    swap = pltpu.make_async_remote_copy(
-        src_ref=weights,
-        dst_ref=other_w,
-        send_sem=swap_sems.at[0],
-        recv_sem=swap_sems.at[1],
-        device_id=(group, me, 1 - core),
-        device_id_type=mesh_ids,
-    )
-    swap.start()
-    sends = [swap]
+    parts = SWAP_PARTS
+    depth = weights.shape[0] // parts
+    swaps = []
+    for part in range(parts):
+        rows_part = pl.ds(part * depth, depth)
+        swap = pltpu.make_async_remote_copy(
+            src_ref=weights.at[rows_part],
+            dst_ref=other_w.at[rows_part],
+            send_sem=swap_sems.at[part],
+            recv_sem=swap_sems.at[parts + part],
+            device_id=(group, me, 1 - core),
+            device_id_type=mesh_ids,
+        )
+        swap.start()
+        swaps.append(swap)
+    sends = list(swaps)
     for shift in range(1, count):
         peer = lax.rem(me + shift, count)
         copy = pltpu.make_async_remote_copy(
@@ -210,7 +217,8 @@
         copy.start()
         sends.append(copy)
     load_w.wait()
-    swap.wait_recv()
+    for swap in swaps:
+        swap.wait_recv()
     load_x.wait()
     outs = []
     for shift in range(count):
@@ -285,7 +293,7 @@
             pltpu.SemaphoreType.DMA((count,)),
             pltpu.SemaphoreType.DMA((count,)),
             pltpu.SemaphoreType.DMA((count,)),
-            pltpu.SemaphoreType.DMA((2,)),
+            pltpu.SemaphoreType.DMA((2 * SWAP_PARTS,)),
             pltpu.SemaphoreType.DMA((3,)),
         ],
         compiler_params=pltpu.CompilerParams(

time: 300 us -> 300 us (level)
  no operation moved by 1% of the time
where the time goes in v7:
time: 300 us; the launch traced here: 294 us
  Pallas kernels  202 us (67%)
  other arithmetic  27.1 us (9%)
  matrix products  20.5 us (7%)
  between operations  14.9 us (5%)
  waiting for transfers between devices  13.4 us (4%)
  local copies, waits for them, and re-layouts  12.9 us (4%)
    pallas_call x2, Pallas kernels, exchange(): pl.pallas_call(functools.partial(exchange_kernel, count, spread, spreads,...  106 us
    pallas_call x1, Pallas kernels, fused_mlp(): pl.pallas_call(functools.partial(mlp_kernel, count, ff), out_shape=jax.Sh...  96.4 us
    ppermute x1, waiting for transfers between devices, from_behind(): return lax.ppermute(block, axis, route)  13 us
    sub x1, matrix products, body(): probs = jnp.where(visible[None], jnp.exp(scores - row_peak), 0.0)  10.4 us
    scatter x1, local copies, waits for them, and re-layouts, body(): jnp.zeros((pages * PAGE, width), jnp.bfloat16).at[target].set(own_slice)  6.12 us
  transfers between devices with their start and end apart: 5, of which 2 were waited for; matrix products, arithmetic and copies ran while one was open for 18% of the time, Pallas kernels for 36%

profile of v7, /device:TPU:2, one launch (start us, length us, event | category | flops | bytes accessed | tf_op | source)
XLA Modules:
  0.0 293.7 jit_solution(16281225810806639348)
XLA Ops:
  7.3 1.0 convert_bitcast_fusion.1
  8.2 1.0 copy.33
  9.2 0.8 convert_element_type.94
  11.7 1.2 copy.42
  12.9 1.1 convert_element_type.110
  13.9 1.1 convert_element_type.111
  15.0 0.9 pad_maximum_fusion.1
  17.3 0.9 fusion.31.refs_0_
  18.2 57.2 %shard_map.140 = bf16[8,96,2048]{2,1,0:T(8,128)(2,1)} custom-call(bf16[96,2048]{1,0:T(8,128)(2,1)} %fusion.31.refs_0_), custom_call_target="tpu_custom_call" | custom-call | bytes 6291456 | tf_op jit(solution)/shard_map/pallas_call | solution.py:144
  78.0 2.5 multiply_cosine_fusion
  80.6 1.4 compare_and_fusion
  82.0 1.7 pad_add_fusion
  84.4 1.2 fusion.19
  86.4 1.2 fusion.20
  88.3 0.9 fusion.72
  89.1 1.0 convolution_convert_fusion.1
  90.8 1.2 broadcast_select_fusion.1
  92.0 0.9 copy.35
  93.1 1.1 pad_maximum_fusion
  94.3 1.9 collective-permute-start.2
  96.3 2.2 subtract_convert_fusion
  98.5 6.1 %scatter_custom_fusion = bf16[8192,128]{1,0:T(8,128)(2,1)} fusion(s32[1536]{0:T(1024)S(1)} %compare_select_fusion, bf16[]{:T(256)} %constant.67.clone.1, bf16[1536,2,128]{2,0,1:T(8,128)(2,1)S(1)} %bitcast.81, s32[]{:T(128)} %constant.56.clone.1, s32[]{:T(128)S(6)} %select_n.66), kind=kCustom, calls=%fused_computation.36 | custom fusion | bytes 2490378 | tf_op jit(solution)/shard_map/scatter | solution.py:453
  104.6 13.0 %collective-permute-done.2 = bf16[512,2,128]{2,0,1:T(8,128)(2,1)} collective-permute-done((bf16[512,2,128]{2,0,1:T(8,128)(2,1)S(1)}, bf16[512,2,128]{2,0,1:T(8,128)(2,1)}, u32[]{:S(2)}, u32[]{:S(2)}) %collective-permute-start.2) | collective-permute-done | bytes 262176 | tf_op jit(solution)/shard_map/ppermute | solution.py:30
  117.6 10.4 %fusion.74 = (f32[2,768]{1,0:T(2,128)S(1)}, bf16[2,768,2048]{1,2,0:T(8,128)(2,1)}) fusion(pred[768,2048]{0,1:T(8,128)(4,1)} %pad_add_fusion, bf16[1536,2,128]{2,0,1:T(8,128)(2,1)S(1)} %bitcast.82, bf16[512,2,128]{2,0,1:T(8,128)(2,1)} %collective-permute-done.2, bf16[768,2,64]{2,0,1:T(8,128)(2,1)} %get-tuple-element.7, bf16[768,2,64]{2,0,1:T(8,128)(2,1)} %get-tuple-element.6), kind=kOutput, calls=%fused_computation.115 | convolution fusion | flops 826017792 | bytes 9312256 | tf_op jit(solution)/shard_map/sub | solution.py:430
  128.0 4.0 %fusion.15 = bf16[768,2,128]{0,2,1:T(8,128)(2,1)S(1)} fusion(bf16[2,768,2048]{1,2,0:T(8,128)(2,1)} %get-tuple-element.21, bf16[512,2,128]{2,0,1:T(8,128)(2,1)} %collective-permute-done.2, bf16[1536,2,128]{2,0,1:T(8,128)(2,1)S(1)} %bitcast.83, f32[768,2]{0,1:T(2,128)S(1)} %bitcast.91), kind=kOutput, calls=%fused_computation.18 | convolution fusion | flops 806748160 | bytes 7739392 | tf_op jit(solution)/shard_map/hqk,kd->qhd/dot_general | solution.py:432
  132.0 2.7 convolution_convert_fusion
  134.7 48.6 %shard_map.141 = bf16[8,96,2048]{2,1,0:T(8,128)(2,1)} custom-call(bf16[8,96,2048]{2,1,0:T(8,128)(2,1)} %bitcast.76), custom_call_target="tpu_custom_call" | custom-call | bytes 6291456 | tf_op jit(solution)/shard_map/pallas_call | solution.py:144
  183.3 2.5 convert_reduce_fusion.1
  186.1 0.9 multiply_convert_fusion.own_block
  187.0 96.4 %shard_map.142 = bf16[8,96,2048]{2,1,0:T(8,128)(2,1)} custom-call(bf16[96,2048]{1,0:T(8,128)(2,1)} %multiply_convert_fusion.own_block, bf16[2048,1536]{1,0:T(8,128)(2,1)} %all-gather.5.cloned.1.call-done.weights), custom_call_target="tpu_custom_call" | custom-call | flops 9663676416 | bytes 12582912 | tf_op jit(solution)/shard_map/pallas_call | solution.py:282
  283.4 2.5 convert_reduce_fusion
  286.0 0.9 add_convert_fusion
  (67 shorter events, 8.3 us)
Async XLA Ops:
  7.2 8.8 %copy-start.6 = (s32[1536]{0:T(1024)S(1)}, s32[1536]{0:T(1024)}, u32[]{:S(2)}) copy-start(s32[1536]{0:T(1024)} %param.14) | copy-start | bytes 18436
  7.2 9.4 %copy-start.5 = (s32[1536]{0:T(1024)S(1)}, s32[1536]{0:T(1024)}, u32[]{:S(2)}) copy-start(s32[1536]{0:T(1024)} %param.15) | copy-start | bytes 18436
  7.2 10.0 %copy-start = (bf16[96,2048]{1,0:T(8,128)(2,1)S(1)}, bf16[96,2048]{1,0:T(8,128)(2,1)}, u32[]{:S(2)}) copy-start(bf16[96,2048]{1,0:T(8,128)(2,1)} %param.13) | copy-start | bytes 1179652
  7.2 10.1 %copy-start.7 = (f32[2048]{0:T(1024)S(1)}, f32[2048]{0:T(1024)}, u32[]{:S(2)}) copy-start(f32[2048]{0:T(1024)} %param.17) | copy-start | bytes 24580
  7.2 73.3 %all-gather.3.cloned.1.call-start = ((), (), s32[]{:S(2)}) async-start(), calls=%async_computation | async-start | bytes 1769472 | tf_op jit(solution)/shard_map/all_gather | solution.py:382
  11.6 175.3 %all-gather.5.cloned.1.call-start = ((), (), s32[]{:S(2)}) async-start(), calls=%async_computation.1 | async-start | bytes 7077888 | tf_op jit(solution)/shard_map/all_gather | solution.py:398
  15.9 61.1 %copy-start.9 = (s32[1,64]{1,0:T(1,128)S(1)}, s32[1,64]{1,0:T(1,128)}, u32[]{:S(2)}) copy-start(s32[1,64]{1,0:T(1,128)} %param.16) | copy-start | bytes 772
  80.5 3.2 %copy-start.3 = (bf16[2048,384]{0,1:T(8,128)(2,1)S(1)}, bf16[2048,384]{0,1:T(8,128)(2,1)}, u32[]{:S(2)}) copy-start(bf16[2048,384]{0,1:T(8,128)(2,1)} %all-gather.3.cloned.1.call-done) | copy-start | bytes 4718596
  80.5 3.6 %collective-permute-start = (bf16[2048,384]{0,1:T(8,128)(2,1)}, bf16[2048,384]{0,1:T(8,128)(2,1)S(1)}, u32[]{:S(2)}, u32[]{:S(2)}) collective-permute-start(bf16[2048,384]{0,1:T(8,128)(2,1)} %all-gather.3.cloned.1.call-done), channel_id=1, source_target_pairs={{0,1},{1,0},{2,3},{3,2},{4,5},{5,4},{6,7},{7,6},{8,9},{9,8},{10,11... | collective-permute-start | bytes 4718600 | tf_op jit(solution)/shard_map/ppermute | solution.py:24
  82.0 2.5 copy-start.1
  87.6 2.6 copy-start.4
  87.7 3.1 %collective-permute-start.1 = (bf16[768,2,128]{0,2,1:T(8,128)(2,1)S(1)}, bf16[768,2,128]{0,2,1:T(8,128)(2,1)}, u32[]{:S(2)}, u32[]{:S(2)}) collective-permute-start(bf16[768,2,128]{0,2,1:T(8,128)(2,1)S(1)} %pad_maximum_fusion.3), channel_id=1, source_target_pairs={{0,1},{1,0},{2,3},{3,2},{4,5},{5,4},{6,7},{7,6},{8,9},{9,8},{10,11... | collective-permute-start | bytes 1179656 | tf_op jit(solution)/shard_map/ppermute | solution.py:24
  94.3 23.3 %collective-permute-start.2 = (bf16[512,2,128]{2,0,1:T(8,128)(2,1)S(1)}, bf16[512,2,128]{2,0,1:T(8,128)(2,1)}, u32[]{:S(2)}, u32[]{:S(2)}) collective-permute-start(bf16[512,2,128]{2,0,1:T(8,128)(2,1)S(1)} %slice.91), channel_id=1, source_target_pairs={{0,16},{16,32},{32,48},{48,64},{64,80},{80,96},{96,112},{1,17},{17... | collective-permute-start | bytes 786440 | tf_op jit(solution)/shard_map/ppermute | solution.py:30
  128.0 4.0 %copy-start.2 = (bf16[2048,128]{0,1:T(8,128)(2,1)S(1)}, bf16[2048,128]{0,1:T(8,128)(2,1)}, u32[]{:S(2)}) copy-start(bf16[2048,128]{0,1:T(8,128)(2,1)} %get-tuple-element.10) | copy-start | bytes 1572868
  183.3 2.7 copy-start.8
Sparse Core Ops, SparseCore 0:
  11.7 48.0 all-gather.2
  61.5 84.7 all-gather.4

commit v8 on v4

--- a/solution.py
+++ b/solution.py
@@ -13,6 +13,7 @@
 HD = 128
 PAGE = 128
 MAXLEN = 512
+FAR_FIRST = (4, 2, 6, 3, 5, 1, 7)
 
 
 rope_base = 1000000.0
@@ -27,6 +28,12 @@
     devices = range(lax.axis_size(axis))
     route = [(i - distance, i) for i in devices if i - distance in devices]
     return lax.ppermute(block, axis, route)
+
+
+def send_order(count):
+    if sorted(FAR_FIRST) == list(range(1, count)):
+        return FAR_FIRST
+    return tuple(range(1, count))
 
 
 def exchange_kernel(count, spread, spreads, swaps, *refs):
@@ -86,7 +93,7 @@
             )
             copy.start()
             copies.append(copy)
-    for shift in range(1, count):
+    for shift in send_order(count):
         peer = lax.rem(me + shift, count)
         copy = pltpu.make_async_remote_copy(
             src_ref=source.at[peer] if spread else source,
@@ -197,7 +204,7 @@
     )
     swap.start()
     sends = [swap]
-    for shift in range(1, count):
+    for shift in send_order(count):
         peer = lax.rem(me + shift, count)
         copy = pltpu.make_async_remote_copy(
             src_ref=own_block,

time: 300 us -> 285 us (0.950)
  Pallas kernels: 202 us -> 194 us
  waiting for transfers between devices: 13.4 us -> 8.76 us
    pallas_call x1, Pallas kernels: 96.4 us -> 91 us  [fused_mlp(): pl.pallas_call(functools.partial(mlp_kernel, count, ff), out_shape=jax.Sh...]
    ppermute x1, waiting for transfers between devices: 13 us -> 8.37 us  [from_behind(): return lax.ppermute(block, axis, route)]
  transfers between devices with their start and end apart: 5 -> 5, of which waited for: 2 -> 2; matrix products, arithmetic and copies ran while one was open for 18% -> 19% of each run, Pallas kernels for 36% -> 37%
where the time goes in v8:
time: 285 us; the launch traced here: 281 us
  Pallas kernels  194 us (68%)
  other arithmetic  27.2 us (10%)
  matrix products  20.5 us (7%)
  between operations  14.9 us (5%)
  local copies, waits for them, and re-layouts  12.9 us (5%)
  waiting for transfers between devices  8.76 us (3%)
    pallas_call x2, Pallas kernels, exchange(): pl.pallas_call(functools.partial(exchange_kernel, count, spread, spreads,...  103 us
    pallas_call x1, Pallas kernels, fused_mlp(): pl.pallas_call(functools.partial(mlp_kernel, count, ff), out_shape=jax.Sh...  91 us
    sub x1, matrix products, body(): probs = jnp.where(visible[None], jnp.exp(scores - row_peak), 0.0)  10.4 us
    ppermute x1, waiting for transfers between devices, from_behind(): return lax.ppermute(block, axis, route)  8.37 us
    scatter x1, local copies, waits for them, and re-layouts, body(): jnp.zeros((pages * PAGE, width), jnp.bfloat16).at[target].set(own_slice)  6.12 us
  transfers between devices with their start and end apart: 5, of which 2 were waited for; matrix products, arithmetic and copies ran while one was open for 19% of the time, Pallas kernels for 37%

profile of v8, /device:TPU:2, one launch (start us, length us, event | category | flops | bytes accessed | tf_op | source)
XLA Modules:
  0.0 281.0 jit_solution(11245739315174814059)
XLA Ops:
  7.3 1.0 convert_bitcast_fusion.1
  8.2 1.0 copy.33
  9.2 0.8 convert_element_type.94
  11.7 1.2 copy.42
  12.9 1.1 convert_element_type.110
  13.9 1.1 convert_element_type.111
  15.0 0.9 pad_maximum_fusion.1
  17.3 0.9 fusion.31.refs_0_
  18.2 56.1 %shard_map.140 = bf16[8,96,2048]{2,1,0:T(8,128)(2,1)} custom-call(bf16[96,2048]{1,0:T(8,128)(2,1)} %fusion.31.refs_0_), custom_call_target="tpu_custom_call" | custom-call | bytes 6291456 | tf_op jit(solution)/shard_map/pallas_call | solution.py:150
  77.0 2.5 multiply_cosine_fusion
  79.5 1.4 compare_and_fusion
  80.9 1.7 pad_add_fusion
  83.4 1.2 fusion.19
  85.4 1.2 fusion.20
  87.2 0.9 fusion.72
  88.0 1.0 convolution_convert_fusion.1
  89.7 1.2 broadcast_select_fusion.1
  90.9 0.9 copy.35
  92.0 1.1 pad_maximum_fusion
  93.2 1.9 collective-permute-start.2
  95.2 2.2 subtract_convert_fusion
  97.4 6.1 %scatter_custom_fusion = bf16[8192,128]{1,0:T(8,128)(2,1)} fusion(s32[1536]{0:T(1024)S(1)} %compare_select_fusion, bf16[]{:T(256)} %constant.67.clone.1, bf16[1536,2,128]{2,0,1:T(8,128)(2,1)S(1)} %bitcast.81, s32[]{:T(128)} %constant.56.clone.1, s32[]{:T(128)S(6)} %select_n.66), kind=kCustom, calls=%fused_computation.36 | custom fusion | bytes 2490378 | tf_op jit(solution)/shard_map/scatter | solution.py:452
  103.5 8.4 %collective-permute-done.2 = bf16[512,2,128]{2,0,1:T(8,128)(2,1)} collective-permute-done((bf16[512,2,128]{2,0,1:T(8,128)(2,1)S(1)}, bf16[512,2,128]{2,0,1:T(8,128)(2,1)}, u32[]{:S(2)}, u32[]{:S(2)}) %collective-permute-start.2) | collective-permute-done | bytes 262176 | tf_op jit(solution)/shard_map/ppermute | solution.py:30
  111.9 10.4 %fusion.74 = (f32[2,768]{1,0:T(2,128)S(1)}, bf16[2,768,2048]{1,2,0:T(8,128)(2,1)}) fusion(pred[768,2048]{0,1:T(8,128)(4,1)} %pad_add_fusion, bf16[1536,2,128]{2,0,1:T(8,128)(2,1)S(1)} %bitcast.82, bf16[512,2,128]{2,0,1:T(8,128)(2,1)} %collective-permute-done.2, bf16[768,2,64]{2,0,1:T(8,128)(2,1)} %get-tuple-element.7, bf16[768,2,64]{2,0,1:T(8,128)(2,1)} %get-tuple-element.6), kind=kOutput, calls=%fused_computation.115 | convolution fusion | flops 826017792 | bytes 9312256 | tf_op jit(solution)/shard_map/sub | solution.py:429
  122.2 4.0 %fusion.15 = bf16[768,2,128]{0,2,1:T(8,128)(2,1)S(1)} fusion(bf16[2,768,2048]{1,2,0:T(8,128)(2,1)} %get-tuple-element.21, bf16[512,2,128]{2,0,1:T(8,128)(2,1)} %collective-permute-done.2, bf16[1536,2,128]{2,0,1:T(8,128)(2,1)S(1)} %bitcast.83, f32[768,2]{0,1:T(2,128)S(1)} %bitcast.91), kind=kOutput, calls=%fused_computation.18 | convolution fusion | flops 806748160 | bytes 7739392 | tf_op jit(solution)/shard_map/hqk,kd->qhd/dot_general | solution.py:431
  126.2 2.7 convolution_convert_fusion
  129.0 47.1 %shard_map.141 = bf16[8,96,2048]{2,1,0:T(8,128)(2,1)} custom-call(bf16[8,96,2048]{2,1,0:T(8,128)(2,1)} %bitcast.76), custom_call_target="tpu_custom_call" | custom-call | bytes 6291456 | tf_op jit(solution)/shard_map/pallas_call | solution.py:150
  176.1 2.5 convert_reduce_fusion.1
  178.8 0.9 multiply_convert_fusion.own_block
  179.7 91.0 %shard_map.142 = bf16[8,96,2048]{2,1,0:T(8,128)(2,1)} custom-call(bf16[96,2048]{1,0:T(8,128)(2,1)} %multiply_convert_fusion.own_block, bf16[2048,1536]{1,0:T(8,128)(2,1)} %all-gather.5.cloned.1.call-done.weights), custom_call_target="tpu_custom_call" | custom-call | flops 9663676416 | bytes 12582912 | tf_op jit(solution)/shard_map/pallas_call | solution.py:281
  270.7 2.5 convert_reduce_fusion
  273.3 0.9 add_convert_fusion
  (67 shorter events, 8.2 us)
Async XLA Ops:
  7.2 8.8 %copy-start.6 = (s32[1536]{0:T(1024)S(1)}, s32[1536]{0:T(1024)}, u32[]{:S(2)}) copy-start(s32[1536]{0:T(1024)} %param.14) | copy-start | bytes 18436
  7.2 9.4 %copy-start.5 = (s32[1536]{0:T(1024)S(1)}, s32[1536]{0:T(1024)}, u32[]{:S(2)}) copy-start(s32[1536]{0:T(1024)} %param.15) | copy-start | bytes 18436
  7.2 10.0 %copy-start = (bf16[96,2048]{1,0:T(8,128)(2,1)S(1)}, bf16[96,2048]{1,0:T(8,128)(2,1)}, u32[]{:S(2)}) copy-start(bf16[96,2048]{1,0:T(8,128)(2,1)} %param.13) | copy-start | bytes 1179652
  7.2 10.1 %copy-start.7 = (f32[2048]{0:T(1024)S(1)}, f32[2048]{0:T(1024)}, u32[]{:S(2)}) copy-start(f32[2048]{0:T(1024)} %param.17) | copy-start | bytes 24580
  7.2 72.2 %all-gather.3.cloned.1.call-start = ((), (), s32[]{:S(2)}) async-start(), calls=%async_computation | async-start | bytes 1769472 | tf_op jit(solution)/shard_map/all_gather | solution.py:381
  11.6 168.1 %all-gather.5.cloned.1.call-start = ((), (), s32[]{:S(2)}) async-start(), calls=%async_computation.1 | async-start | bytes 7077888 | tf_op jit(solution)/shard_map/all_gather | solution.py:397
  15.9 60.0 %copy-start.9 = (s32[1,64]{1,0:T(1,128)S(1)}, s32[1,64]{1,0:T(1,128)}, u32[]{:S(2)}) copy-start(s32[1,64]{1,0:T(1,128)} %param.16) | copy-start | bytes 772
  79.5 3.2 %copy-start.3 = (bf16[2048,384]{0,1:T(8,128)(2,1)S(1)}, bf16[2048,384]{0,1:T(8,128)(2,1)}, u32[]{:S(2)}) copy-start(bf16[2048,384]{0,1:T(8,128)(2,1)} %all-gather.3.cloned.1.call-done) | copy-start | bytes 4718596
  79.5 3.6 %collective-permute-start = (bf16[2048,384]{0,1:T(8,128)(2,1)}, bf16[2048,384]{0,1:T(8,128)(2,1)S(1)}, u32[]{:S(2)}, u32[]{:S(2)}) collective-permute-start(bf16[2048,384]{0,1:T(8,128)(2,1)} %all-gather.3.cloned.1.call-done), channel_id=1, source_target_pairs={{0,1},{1,0},{2,3},{3,2},{4,5},{5,4},{6,7},{7,6},{8,9},{9,8},{10,11... | collective-permute-start | bytes 4718600 | tf_op jit(solution)/shard_map/ppermute | solution.py:24
  80.9 2.5 copy-start.1
  86.5 2.5 copy-start.4
  86.6 3.1 %collective-permute-start.1 = (bf16[768,2,128]{0,2,1:T(8,128)(2,1)S(1)}, bf16[768,2,128]{0,2,1:T(8,128)(2,1)}, u32[]{:S(2)}, u32[]{:S(2)}) collective-permute-start(bf16[768,2,128]{0,2,1:T(8,128)(2,1)S(1)} %pad_maximum_fusion.3), channel_id=1, source_target_pairs={{0,1},{1,0},{2,3},{3,2},{4,5},{5,4},{6,7},{7,6},{8,9},{9,8},{10,11... | collective-permute-start | bytes 1179656 | tf_op jit(solution)/shard_map/ppermute | solution.py:24
  93.2 18.6 %collective-permute-start.2 = (bf16[512,2,128]{2,0,1:T(8,128)(2,1)S(1)}, bf16[512,2,128]{2,0,1:T(8,128)(2,1)}, u32[]{:S(2)}, u32[]{:S(2)}) collective-permute-start(bf16[512,2,128]{2,0,1:T(8,128)(2,1)S(1)} %slice.91), channel_id=1, source_target_pairs={{0,16},{16,32},{32,48},{48,64},{64,80},{80,96},{96,112},{1,17},{17... | collective-permute-start | bytes 786440 | tf_op jit(solution)/shard_map/ppermute | solution.py:30
  122.2 4.0 %copy-start.2 = (bf16[2048,128]{0,1:T(8,128)(2,1)S(1)}, bf16[2048,128]{0,1:T(8,128)(2,1)}, u32[]{:S(2)}) copy-start(bf16[2048,128]{0,1:T(8,128)(2,1)} %get-tuple-element.10) | copy-start | bytes 1572868
  176.1 2.7 copy-start.8
Sparse Core Ops, SparseCore 0:
  11.7 48.1 all-gather.2
  61.5 90.8 all-gather.4

commit v9 on v8

--- a/solution.py
+++ b/solution.py
@@ -220,7 +220,7 @@
     swap.wait_recv()
     load_x.wait()
     outs = []
-    for shift in range(count):
+    for shift in (0,) + send_order(count):
         sender = lax.rem(me + count - shift, count)
         if shift > 0:
             pltpu.make_async_remote_copy(

time: 285 us -> 267 us (0.937)
  Pallas kernels: 194 us -> 178 us
    pallas_call x1, Pallas kernels: 91 us -> 74.5 us  [fused_mlp(): pl.pallas_call(functools.partial(mlp_kernel, count, ff), out_shape=jax.Sh...]
  transfers between devices with their start and end apart: 5 -> 5, of which waited for: 2 -> 2; matrix products, arithmetic and copies ran while one was open for 19% -> 20% of each run, Pallas kernels for 37% -> 39%
where the time goes in v9:
time: 267 us; the launch traced here: 264 us
  Pallas kernels  178 us (67%)
  other arithmetic  27.2 us (10%)
  matrix products  20.5 us (8%)
  between operations  14.9 us (6%)
  local copies, waits for them, and re-layouts  12.9 us (5%)
  waiting for transfers between devices  8.76 us (3%)
    pallas_call x2, Pallas kernels, exchange(): pl.pallas_call(functools.partial(exchange_kernel, count, spread, spreads,...  103 us
    pallas_call x1, Pallas kernels, fused_mlp(): pl.pallas_call(functools.partial(mlp_kernel, count, ff), out_shape=jax.Sh...  74.5 us
    sub x1, matrix products, body(): probs = jnp.where(visible[None], jnp.exp(scores - row_peak), 0.0)  10.4 us
    ppermute x1, waiting for transfers between devices, from_behind(): return lax.ppermute(block, axis, route)  8.37 us
    scatter x1, local copies, waits for them, and re-layouts, body(): jnp.zeros((pages * PAGE, width), jnp.bfloat16).at[target].set(own_slice)  6.12 us
  transfers between devices with their start and end apart: 5, of which 2 were waited for; matrix products, arithmetic and copies ran while one was open for 20% of the time, Pallas kernels for 39%

profile of v9, /device:TPU:2, one launch (start us, length us, event | category | flops | bytes accessed | tf_op | source)
XLA Modules:
  0.0 264.5 jit_solution(1438000470897062535)
XLA Ops:
  7.3 1.0 convert_bitcast_fusion.1
  8.2 1.0 copy.33
  9.2 0.8 convert_element_type.94
  11.7 1.2 copy.42
  12.9 1.1 convert_element_type.110
  13.9 1.1 convert_element_type.111
  15.0 0.9 pad_maximum_fusion.1
  17.3 0.9 fusion.31.refs_0_
  18.2 56.1 %shard_map.140 = bf16[8,96,2048]{2,1,0:T(8,128)(2,1)} custom-call(bf16[96,2048]{1,0:T(8,128)(2,1)} %fusion.31.refs_0_), custom_call_target="tpu_custom_call" | custom-call | bytes 6291456 | tf_op jit(solution)/shard_map/pallas_call | solution.py:150
  77.0 2.5 multiply_cosine_fusion
  79.5 1.4 compare_and_fusion
  80.9 1.7 pad_add_fusion
  83.4 1.2 fusion.19
  85.4 1.2 fusion.20
  87.2 0.9 fusion.72
  88.0 1.0 convolution_convert_fusion.1
  89.7 1.2 broadcast_select_fusion.1
  90.9 0.9 copy.35
  92.0 1.1 pad_maximum_fusion
  93.2 1.9 collective-permute-start.2
  95.2 2.2 subtract_convert_fusion
  97.4 6.1 %scatter_custom_fusion = bf16[8192,128]{1,0:T(8,128)(2,1)} fusion(s32[1536]{0:T(1024)S(1)} %compare_select_fusion, bf16[]{:T(256)} %constant.67.clone.1, bf16[1536,2,128]{2,0,1:T(8,128)(2,1)S(1)} %bitcast.81, s32[]{:T(128)} %constant.56.clone.1, s32[]{:T(128)S(6)} %select_n.66), kind=kCustom, calls=%fused_computation.36 | custom fusion | bytes 2490378 | tf_op jit(solution)/shard_map/scatter | solution.py:452
  103.5 8.4 %collective-permute-done.2 = bf16[512,2,128]{2,0,1:T(8,128)(2,1)} collective-permute-done((bf16[512,2,128]{2,0,1:T(8,128)(2,1)S(1)}, bf16[512,2,128]{2,0,1:T(8,128)(2,1)}, u32[]{:S(2)}, u32[]{:S(2)}) %collective-permute-start.2) | collective-permute-done | bytes 262176 | tf_op jit(solution)/shard_map/ppermute | solution.py:30
  111.9 10.4 %fusion.74 = (f32[2,768]{1,0:T(2,128)S(1)}, bf16[2,768,2048]{1,2,0:T(8,128)(2,1)}) fusion(pred[768,2048]{0,1:T(8,128)(4,1)} %pad_add_fusion, bf16[1536,2,128]{2,0,1:T(8,128)(2,1)S(1)} %bitcast.82, bf16[512,2,128]{2,0,1:T(8,128)(2,1)} %collective-permute-done.2, bf16[768,2,64]{2,0,1:T(8,128)(2,1)} %get-tuple-element.7, bf16[768,2,64]{2,0,1:T(8,128)(2,1)} %get-tuple-element.6), kind=kOutput, calls=%fused_computation.115 | convolution fusion | flops 826017792 | bytes 9312256 | tf_op jit(solution)/shard_map/sub | solution.py:429
  122.2 4.0 %fusion.15 = bf16[768,2,128]{0,2,1:T(8,128)(2,1)S(1)} fusion(bf16[2,768,2048]{1,2,0:T(8,128)(2,1)} %get-tuple-element.21, bf16[512,2,128]{2,0,1:T(8,128)(2,1)} %collective-permute-done.2, bf16[1536,2,128]{2,0,1:T(8,128)(2,1)S(1)} %bitcast.83, f32[768,2]{0,1:T(2,128)S(1)} %bitcast.91), kind=kOutput, calls=%fused_computation.18 | convolution fusion | flops 806748160 | bytes 7739392 | tf_op jit(solution)/shard_map/hqk,kd->qhd/dot_general | solution.py:431
  126.2 2.7 %convolution_convert_fusion = bf16[768,2048]{1,0:T(8,128)(2,1)} fusion(bf16[768,256]{0,1:T(8,128)(2,1)S(1)} %bitcast.89, bf16[2048,128]{0,1:T(8,128)(2,1)S(1)} %copy-done.2, bf16[2048,128]{0,1:T(8,128)(2,1)S(1)} %get-tuple-element.8), kind=kOutput, calls=%fused_computation.14 | convolution fusion | flops 808976384 | bytes 4587520 | tf_op jit(solution)/shard_map/dot_general | solution.py:347
  129.0 47.1 %shard_map.141 = bf16[8,96,2048]{2,1,0:T(8,128)(2,1)} custom-call(bf16[8,96,2048]{2,1,0:T(8,128)(2,1)} %bitcast.76), custom_call_target="tpu_custom_call" | custom-call | bytes 6291456 | tf_op jit(solution)/shard_map/pallas_call | solution.py:150
  176.1 2.5 convert_reduce_fusion.1
  178.8 0.9 multiply_convert_fusion.own_block
  179.7 74.5 %shard_map.142 = bf16[8,96,2048]{2,1,0:T(8,128)(2,1)} custom-call(bf16[96,2048]{1,0:T(8,128)(2,1)} %multiply_convert_fusion.own_block, bf16[2048,1536]{1,0:T(8,128)(2,1)} %all-gather.5.cloned.1.call-done.weights), custom_call_target="tpu_custom_call" | custom-call | flops 9663676416 | bytes 12582912 | tf_op jit(solution)/shard_map/pallas_call | solution.py:281
  254.2 2.5 convert_reduce_fusion
  256.7 0.9 add_convert_fusion
  (67 shorter events, 8.2 us)
Async XLA Ops:
  7.2 8.8 %copy-start.6 = (s32[1536]{0:T(1024)S(1)}, s32[1536]{0:T(1024)}, u32[]{:S(2)}) copy-start(s32[1536]{0:T(1024)} %param.14) | copy-start | bytes 18436
  7.2 9.4 %copy-start.5 = (s32[1536]{0:T(1024)S(1)}, s32[1536]{0:T(1024)}, u32[]{:S(2)}) copy-start(s32[1536]{0:T(1024)} %param.15) | copy-start | bytes 18436
  7.2 10.0 %copy-start = (bf16[96,2048]{1,0:T(8,128)(2,1)S(1)}, bf16[96,2048]{1,0:T(8,128)(2,1)}, u32[]{:S(2)}) copy-start(bf16[96,2048]{1,0:T(8,128)(2,1)} %param.13) | copy-start | bytes 1179652
  7.2 10.1 %copy-start.7 = (f32[2048]{0:T(1024)S(1)}, f32[2048]{0:T(1024)}, u32[]{:S(2)}) copy-start(f32[2048]{0:T(1024)} %param.17) | copy-start | bytes 24580
  7.2 72.2 %all-gather.3.cloned.1.call-start = ((), (), s32[]{:S(2)}) async-start(), calls=%async_computation | async-start | bytes 1769472 | tf_op jit(solution)/shard_map/all_gather | solution.py:381
  11.6 168.1 %all-gather.5.cloned.1.call-start = ((), (), s32[]{:S(2)}) async-start(), calls=%async_computation.1 | async-start | bytes 7077888 | tf_op jit(solution)/shard_map/all_gather | solution.py:397
  15.9 60.0 %copy-start.9 = (s32[1,64]{1,0:T(1,128)S(1)}, s32[1,64]{1,0:T(1,128)}, u32[]{:S(2)}) copy-start(s32[1,64]{1,0:T(1,128)} %param.16) | copy-start | bytes 772
  79.5 3.2 %copy-start.3 = (bf16[2048,384]{0,1:T(8,128)(2,1)S(1)}, bf16[2048,384]{0,1:T(8,128)(2,1)}, u32[]{:S(2)}) copy-start(bf16[2048,384]{0,1:T(8,128)(2,1)} %all-gather.3.cloned.1.call-done) | copy-start | bytes 4718596
  79.5 3.6 %collective-permute-start = (bf16[2048,384]{0,1:T(8,128)(2,1)}, bf16[2048,384]{0,1:T(8,128)(2,1)S(1)}, u32[]{:S(2)}, u32[]{:S(2)}) collective-permute-start(bf16[2048,384]{0,1:T(8,128)(2,1)} %all-gather.3.cloned.1.call-done), channel_id=1, source_target_pairs={{0,1},{1,0},{2,3},{3,2},{4,5},{5,4},{6,7},{7,6},{8,9},{9,8},{10,11... | collective-permute-start | bytes 4718600 | tf_op jit(solution)/shard_map/ppermute | solution.py:24
  80.9 2.5 copy-start.1
  86.5 2.5 copy-start.4
  86.6 3.1 %collective-permute-start.1 = (bf16[768,2,128]{0,2,1:T(8,128)(2,1)S(1)}, bf16[768,2,128]{0,2,1:T(8,128)(2,1)}, u32[]{:S(2)}, u32[]{:S(2)}) collective-permute-start(bf16[768,2,128]{0,2,1:T(8,128)(2,1)S(1)} %pad_maximum_fusion.3), channel_id=1, source_target_pairs={{0,1},{1,0},{2,3},{3,2},{4,5},{5,4},{6,7},{7,6},{8,9},{9,8},{10,11... | collective-permute-start | bytes 1179656 | tf_op jit(solution)/shard_map/ppermute | solution.py:24
  93.2 18.6 %collective-permute-start.2 = (bf16[512,2,128]{2,0,1:T(8,128)(2,1)S(1)}, bf16[512,2,128]{2,0,1:T(8,128)(2,1)}, u32[]{:S(2)}, u32[]{:S(2)}) collective-permute-start(bf16[512,2,128]{2,0,1:T(8,128)(2,1)S(1)} %slice.91), channel_id=1, source_target_pairs={{0,16},{16,32},{32,48},{48,64},{64,80},{80,96},{96,112},{1,17},{17... | collective-permute-start | bytes 786440 | tf_op jit(solution)/shard_map/ppermute | solution.py:30
  122.2 4.0 %copy-start.2 = (bf16[2048,128]{0,1:T(8,128)(2,1)S(1)}, bf16[2048,128]{0,1:T(8,128)(2,1)}, u32[]{:S(2)}) copy-start(bf16[2048,128]{0,1:T(8,128)(2,1)} %get-tuple-element.10) | copy-start | bytes 1572868
  176.1 2.7 %copy-start.8 = (f32[2048]{0:T(1024)S(1)}, f32[2048]{0:T(1024)}, u32[]{:S(2)}) copy-start(f32[2048]{0:T(1024)} %param.18) | copy-start | bytes 24580
Sparse Core Ops, SparseCore 0:
  11.7 48.1 all-gather.2
  61.5 90.8 all-gather.4

commit v10 on v9

--- a/solution.py
+++ b/solution.py
@@ -62,9 +62,7 @@
             pl.semaphore_signal(barrier, inc=1, device_id=(peer, me, core), device_id_type=mesh_ids)
         greeted += groups - 1
     pl.semaphore_wait(barrier, greeted)
-    local = pltpu.make_async_copy(source.at[me] if spread else source, slots.at[me], local_sem.at[0])
-    local.start()
-    locals_ = [local]
+    locals_ = []
     copies = []
     if swaps:
         swap = pltpu.make_async_remote_copy(
@@ -105,6 +103,9 @@
         )
         copy.start()
         copies.append(copy)
+    local = pltpu.make_async_copy(source.at[me] if spread else source, slots.at[me], local_sem.at[0])
+    local.start()
+    locals_.append(local)
     for shift in range(1, count):
         sender = lax.rem(me + count - shift, count)
         pltpu.make_async_remote_copy(

time: 267 us -> 267 us (level)
  no operation moved by 1% of the time
where the time goes in v10:
time: 267 us; the launch traced here: 264 us
  Pallas kernels  178 us (67%)
  other arithmetic  27.2 us (10%)
  matrix products  20.5 us (8%)
  between operations  14.9 us (6%)
  local copies, waits for them, and re-layouts  12.9 us (5%)
  waiting for transfers between devices  8.76 us (3%)
    pallas_call x2, Pallas kernels, exchange(): pl.pallas_call(functools.partial(exchange_kernel, count, spread, spreads,...  103 us
    pallas_call x1, Pallas kernels, fused_mlp(): pl.pallas_call(functools.partial(mlp_kernel, count, ff), out_shape=jax.Sh...  74.5 us
    sub x1, matrix products, body(): probs = jnp.where(visible[None], jnp.exp(scores - row_peak), 0.0)  10.4 us
    ppermute x1, waiting for transfers between devices, from_behind(): return lax.ppermute(block, axis, route)  8.37 us
    scatter x1, local copies, waits for them, and re-layouts, body(): jnp.zeros((pages * PAGE, width), jnp.bfloat16).at[target].set(own_slice)  6.12 us
  transfers between devices with their start and end apart: 5, of which 2 were waited for; matrix products, arithmetic and copies ran while one was open for 20% of the time, Pallas kernels for 39%

profile of v10, /device:TPU:2, one launch (start us, length us, event | category | flops | bytes accessed | tf_op | source)
XLA Modules:
  0.0 264.5 jit_solution(4916531387523585666)
XLA Ops:
  7.3 1.0 convert_bitcast_fusion.1
  8.2 1.0 copy.33
  9.2 0.8 convert_element_type.94
  11.7 1.2 copy.42
  12.9 1.1 convert_element_type.110
  13.9 1.1 convert_element_type.111
  15.0 0.9 pad_maximum_fusion.1
  17.3 0.9 fusion.31.refs_0_
  18.2 56.1 %shard_map.140 = bf16[8,96,2048]{2,1,0:T(8,128)(2,1)} custom-call(bf16[96,2048]{1,0:T(8,128)(2,1)} %fusion.31.refs_0_), custom_call_target="tpu_custom_call" | custom-call | bytes 6291456 | tf_op jit(solution)/shard_map/pallas_call | solution.py:151
  77.0 2.5 multiply_cosine_fusion
  79.5 1.4 compare_and_fusion
  80.9 1.7 pad_add_fusion
  83.4 1.2 fusion.19
  85.4 1.2 fusion.20
  87.2 0.9 fusion.72
  88.0 1.0 convolution_convert_fusion.1
  89.7 1.2 broadcast_select_fusion.1
  90.9 0.9 copy.35
  92.0 1.1 pad_maximum_fusion
  93.2 1.9 collective-permute-start.2
  95.2 2.2 subtract_convert_fusion
  97.4 6.1 %scatter_custom_fusion = bf16[8192,128]{1,0:T(8,128)(2,1)} fusion(s32[1536]{0:T(1024)S(1)} %compare_select_fusion, bf16[]{:T(256)} %constant.67.clone.1, bf16[1536,2,128]{2,0,1:T(8,128)(2,1)S(1)} %bitcast.81, s32[]{:T(128)} %constant.56.clone.1, s32[]{:T(128)S(6)} %select_n.66), kind=kCustom, calls=%fused_computation.36 | custom fusion | bytes 2490378 | tf_op jit(solution)/shard_map/scatter | solution.py:453
  103.5 8.4 %collective-permute-done.2 = bf16[512,2,128]{2,0,1:T(8,128)(2,1)} collective-permute-done((bf16[512,2,128]{2,0,1:T(8,128)(2,1)S(1)}, bf16[512,2,128]{2,0,1:T(8,128)(2,1)}, u32[]{:S(2)}, u32[]{:S(2)}) %collective-permute-start.2) | collective-permute-done | bytes 262176 | tf_op jit(solution)/shard_map/ppermute | solution.py:30
  111.9 10.4 %fusion.74 = (f32[2,768]{1,0:T(2,128)S(1)}, bf16[2,768,2048]{1,2,0:T(8,128)(2,1)}) fusion(pred[768,2048]{0,1:T(8,128)(4,1)} %pad_add_fusion, bf16[1536,2,128]{2,0,1:T(8,128)(2,1)S(1)} %bitcast.82, bf16[512,2,128]{2,0,1:T(8,128)(2,1)} %collective-permute-done.2, bf16[768,2,64]{2,0,1:T(8,128)(2,1)} %get-tuple-element.7, bf16[768,2,64]{2,0,1:T(8,128)(2,1)} %get-tuple-element.6), kind=kOutput, calls=%fused_computation.115 | convolution fusion | flops 826017792 | bytes 9312256 | tf_op jit(solution)/shard_map/sub | solution.py:430
  122.2 4.0 %fusion.15 = bf16[768,2,128]{0,2,1:T(8,128)(2,1)S(1)} fusion(bf16[2,768,2048]{1,2,0:T(8,128)(2,1)} %get-tuple-element.21, bf16[512,2,128]{2,0,1:T(8,128)(2,1)} %collective-permute-done.2, bf16[1536,2,128]{2,0,1:T(8,128)(2,1)S(1)} %bitcast.83, f32[768,2]{0,1:T(2,128)S(1)} %bitcast.91), kind=kOutput, calls=%fused_computation.18 | convolution fusion | flops 806748160 | bytes 7739392 | tf_op jit(solution)/shard_map/hqk,kd->qhd/dot_general | solution.py:432
  126.3 2.7 %convolution_convert_fusion = bf16[768,2048]{1,0:T(8,128)(2,1)} fusion(bf16[768,256]{0,1:T(8,128)(2,1)S(1)} %bitcast.89, bf16[2048,128]{0,1:T(8,128)(2,1)S(1)} %copy-done.2, bf16[2048,128]{0,1:T(8,128)(2,1)S(1)} %get-tuple-element.8), kind=kOutput, calls=%fused_computation.14 | convolution fusion | flops 808976384 | bytes 4587520 | tf_op jit(solution)/shard_map/dot_general | solution.py:348
  129.0 47.1 %shard_map.141 = bf16[8,96,2048]{2,1,0:T(8,128)(2,1)} custom-call(bf16[8,96,2048]{2,1,0:T(8,128)(2,1)} %bitcast.76), custom_call_target="tpu_custom_call" | custom-call | bytes 6291456 | tf_op jit(solution)/shard_map/pallas_call | solution.py:151
  176.1 2.5 convert_reduce_fusion.1
  178.8 0.9 multiply_convert_fusion.own_block
  179.7 74.5 %shard_map.142 = bf16[8,96,2048]{2,1,0:T(8,128)(2,1)} custom-call(bf16[96,2048]{1,0:T(8,128)(2,1)} %multiply_convert_fusion.own_block, bf16[2048,1536]{1,0:T(8,128)(2,1)} %all-gather.5.cloned.1.call-done.weights), custom_call_target="tpu_custom_call" | custom-call | flops 9663676416 | bytes 12582912 | tf_op jit(solution)/shard_map/pallas_call | solution.py:282
  254.2 2.5 convert_reduce_fusion
  256.7 0.9 add_convert_fusion
  (67 shorter events, 8.2 us)
Async XLA Ops:
  7.2 8.8 %copy-start.6 = (s32[1536]{0:T(1024)S(1)}, s32[1536]{0:T(1024)}, u32[]{:S(2)}) copy-start(s32[1536]{0:T(1024)} %param.14) | copy-start | bytes 18436
  7.2 9.4 %copy-start.5 = (s32[1536]{0:T(1024)S(1)}, s32[1536]{0:T(1024)}, u32[]{:S(2)}) copy-start(s32[1536]{0:T(1024)} %param.15) | copy-start | bytes 18436
  7.2 10.0 %copy-start = (bf16[96,2048]{1,0:T(8,128)(2,1)S(1)}, bf16[96,2048]{1,0:T(8,128)(2,1)}, u32[]{:S(2)}) copy-start(bf16[96,2048]{1,0:T(8,128)(2,1)} %param.13) | copy-start | bytes 1179652
  7.2 10.1 %copy-start.7 = (f32[2048]{0:T(1024)S(1)}, f32[2048]{0:T(1024)}, u32[]{:S(2)}) copy-start(f32[2048]{0:T(1024)} %param.17) | copy-start | bytes 24580
  7.2 72.2 %all-gather.3.cloned.1.call-start = ((), (), s32[]{:S(2)}) async-start(), calls=%async_computation | async-start | bytes 1769472 | tf_op jit(solution)/shard_map/all_gather | solution.py:382
  11.6 168.1 %all-gather.5.cloned.1.call-start = ((), (), s32[]{:S(2)}) async-start(), calls=%async_computation.1 | async-start | bytes 7077888 | tf_op jit(solution)/shard_map/all_gather | solution.py:398
  15.9 60.0 %copy-start.9 = (s32[1,64]{1,0:T(1,128)S(1)}, s32[1,64]{1,0:T(1,128)}, u32[]{:S(2)}) copy-start(s32[1,64]{1,0:T(1,128)} %param.16) | copy-start | bytes 772
  79.5 3.2 %copy-start.3 = (bf16[2048,384]{0,1:T(8,128)(2,1)S(1)}, bf16[2048,384]{0,1:T(8,128)(2,1)}, u32[]{:S(2)}) copy-start(bf16[2048,384]{0,1:T(8,128)(2,1)} %all-gather.3.cloned.1.call-done) | copy-start | bytes 4718596
  79.5 3.6 %collective-permute-start = (bf16[2048,384]{0,1:T(8,128)(2,1)}, bf16[2048,384]{0,1:T(8,128)(2,1)S(1)}, u32[]{:S(2)}, u32[]{:S(2)}) collective-permute-start(bf16[2048,384]{0,1:T(8,128)(2,1)} %all-gather.3.cloned.1.call-done), channel_id=1, source_target_pairs={{0,1},{1,0},{2,3},{3,2},{4,5},{5,4},{6,7},{7,6},{8,9},{9,8},{10,11... | collective-permute-start | bytes 4718600 | tf_op jit(solution)/shard_map/ppermute | solution.py:24
  80.9 2.5 copy-start.1
  86.5 2.5 copy-start.4
  86.6 3.1 %collective-permute-start.1 = (bf16[768,2,128]{0,2,1:T(8,128)(2,1)S(1)}, bf16[768,2,128]{0,2,1:T(8,128)(2,1)}, u32[]{:S(2)}, u32[]{:S(2)}) collective-permute-start(bf16[768,2,128]{0,2,1:T(8,128)(2,1)S(1)} %pad_maximum_fusion.3), channel_id=1, source_target_pairs={{0,1},{1,0},{2,3},{3,2},{4,5},{5,4},{6,7},{7,6},{8,9},{9,8},{10,11... | collective-permute-start | bytes 1179656 | tf_op jit(solution)/shard_map/ppermute | solution.py:24
  93.2 18.6 %collective-permute-start.2 = (bf16[512,2,128]{2,0,1:T(8,128)(2,1)S(1)}, bf16[512,2,128]{2,0,1:T(8,128)(2,1)}, u32[]{:S(2)}, u32[]{:S(2)}) collective-permute-start(bf16[512,2,128]{2,0,1:T(8,128)(2,1)S(1)} %slice.91), channel_id=1, source_target_pairs={{0,16},{16,32},{32,48},{48,64},{64,80},{80,96},{96,112},{1,17},{17... | collective-permute-start | bytes 786440 | tf_op jit(solution)/shard_map/ppermute | solution.py:30
  122.2 4.0 %copy-start.2 = (bf16[2048,128]{0,1:T(8,128)(2,1)S(1)}, bf16[2048,128]{0,1:T(8,128)(2,1)}, u32[]{:S(2)}) copy-start(bf16[2048,128]{0,1:T(8,128)(2,1)} %get-tuple-element.10) | copy-start | bytes 1572868
  176.1 2.7 %copy-start.8 = (f32[2048]{0:T(1024)S(1)}, f32[2048]{0:T(1024)}, u32[]{:S(2)}) copy-start(f32[2048]{0:T(1024)} %param.18) | copy-start | bytes 24580
Sparse Core Ops, SparseCore 0:
  11.7 48.1 all-gather.2
  61.5 90.8 all-gather.4
